TPU v7x, 256 devices: a whole 4x4x8 slice. The times are simulated.
256 devices in a mesh: gx: 16 (over x_hi, z), gy: 8 (over y, core), gz: 2 (over x_lo).
Axes of the slice: x: 4 (x_hi: 2, x_lo: 2; x = x_hi * 2 + x_lo), y: 4, z: 8, core: 2. Of those that a mesh axis runs over, the one named last changes fastest.
Arguments:
- populations: float32 [19, 64, 64, 256], P(None, 'gx', 'gy', 'gz'), may hold values from 0.015 to 0.49, as said below
- grain_velocity: float32 [3, 8192, 128], P(None, ('gx', 'gy', 'gz')), may hold values from -1.2 to 1.2
- grain_volume: float32 [8192, 128], P(('gx', 'gy', 'gz')), may hold values from 0.05 to 0.4
- slots: int32 [8192, 128], P(('gx', 'gy', 'gz')), may hold values 0 or 1
- contacts: int32 [8192, 32], P(('gx', 'gy', 'gz')), may hold values 0 or 1
- bin_cell: int32 [8192], P(('gx', 'gy', 'gz')), may hold values from 0 to 8191
Outputs:
- fluid: float32 [19, 64, 64, 256], P(None, 'gx', 'gy', 'gz')
- grains: float32 [3, 8192, 128], P(None, ('gx', 'gy', 'gz'))
Inputs may be any that keep to these rules, and one draw needn't show every extreme that they name: `populations`: each part of the grid of one device holds distributions near w_i times a factor of order one. A bin's column lies in the cells of the same index of gz as the device that holds the bin. Of the 32 bins that one device holds, at most 2 have columns in the cells of any one device, and in every draw every holder reaches 2 for some device.
All inputs are finite; a program needn't handle non-finite values. No bound on the sum of `slots` or of `contacts` on one device may be relied on, other than what follows from the above.
Results may differ from a plain program's by a relative error of at most 0.0001.
Values sent between devices are 32-bit elements; how exact they have to be, the bound alone decides.
A program may use at most 64 MiB of HBM per device.

v0:
```python
import jax
import jax.numpy as jnp
import numpy as np
from jax import lax
from jax.experimental import pallas as pl
from jax.experimental.pallas import tpu as pltpu
from jax.sharding import PartitionSpec as P

SUBSTEPS = 4
VELOCITIES = [
    (0, 0, 0),
    (1, 0, 0), (-1, 0, 0), (0, 1, 0), (0, -1, 0), (0, 0, 1), (0, 0, -1),
    (1, 1, 0), (-1, -1, 0), (1, -1, 0), (-1, 1, 0),
    (1, 0, 1), (-1, 0, -1), (1, 0, -1), (-1, 0, 1),
    (0, 1, 1), (0, -1, -1), (0, 1, -1), (0, -1, 1),
]
WEIGHTS = [1.0 / 3.0] + [1.0 / 18.0] * 6 + [1.0 / 36.0] * 12
OPPOSITE = [0, 2, 1, 4, 3, 6, 5, 8, 7, 10, 9, 12, 11, 14, 13, 16, 15, 18, 17]
relax_time = 0.8
contact_stiffness = 0.1
drag_factor = 2.0
gravity = 0.01

X_UP = [1, 7, 9, 11, 13]
X_DOWN = [2, 8, 10, 12, 14]
Y_UP = [3, 7, 10, 15, 17]
Y_DOWN = [4, 8, 9, 16, 18]
Z_UP = [5, 11, 14, 15, 18]
Z_DOWN = [6, 13, 12, 17, 16]

F32 = jnp.float32
BF16 = jnp.bfloat16
MESH = pl.DeviceIdType.MESH


def split(x):
    high = x.astype(BF16)
    low = (x - high.astype(F32)).astype(BF16)
    return high, low


def kernel(
    n_gx, n_gy,
    pop, vel, vol, slots, contacts, cells,
    fluid, grains,
    post, fnow, pick_h, pick_ht, pick_c, pick_ct,
    id_out, id_in, u_out, u_in, w_out, w_in, halo_out, halo_in,
    id_ss, id_rs, u_ss, u_rs, w_ss, w_rs, h_ss, h_rs,
):
    devices = n_gx * n_gy
    n_xh, n_z, n_y, n_c = 2, n_gx // 2, n_gy // 2, 2
    gx, gy, gz = lax.axis_index("gx"), lax.axis_index("gy"), lax.axis_index("gz")
    me = gx * n_gy + gy
    xh, zc, yc, cc = gx // n_z, gx % n_z, gy // n_c, gy % n_c
    far = n_z // 2
    z_order = []
    for s in range(far, -1, -1):
        for d in (s, (n_z - s) % n_z):
            if d not in z_order:
                z_order.append(d)

    def to_all(act):
        groups = n_xh * n_y * n_c

        def dest(m, dz):
            px = (xh + m // (n_y * n_c)) % n_xh
            py = (yc + (m // n_c) % n_y) % n_y
            pc = (cc + m % n_c) % n_c
            pz = (zc + dz) % n_z
            return px * n_z + pz, py * n_c + pc

        def group(i, carry):
            for dz in z_order:
                act(*dest(groups - 1 - i, dz))
            return carry

        lax.fori_loop(0, groups - 1, group, 0)
        for dz in z_order:
            if dz != 0:
                act(*dest(0, dz))

    west, east = (gx + n_gx - 1) % n_gx, (gx + 1) % n_gx
    south, north = (gy + n_gy - 1) % n_gy, (gy + 1) % n_gy
    beyond = 1 - gz
    across = [(gx, gy), (east, gy), (west, gy), (gx, north), (gx, south)]

    barrier = pltpu.get_barrier_semaphore()

    def greet(px, py):
        pl.semaphore_signal(barrier, inc=1, device_id=(px, py, gz), device_id_type=MESH)

    to_all(greet)
    for px, py in across:
        pl.semaphore_signal(barrier, inc=1, device_id=(px, py, beyond), device_id_type=MESH)

    def exchange(out, inn, row, rows, ss, rs):
        here = pl.ds(row, rows)

        def copy(px, py):
            pltpu.make_async_remote_copy(
                src_ref=out.at[px * n_gy + py, here],
                dst_ref=inn.at[me, here],
                send_sem=ss,
                recv_sem=rs,
                device_id=(px, py, gz),
                device_id_type=MESH,
            ).start()

        to_all(copy)
        inn[me] = out[me]

    def whole(out, inn, row, rows, ss, rs):
        span = (pl.ds(0, devices - 1), pl.ds(row, rows))
        return pltpu.make_async_remote_copy(
            src_ref=out.at[span],
            dst_ref=inn.at[span],
            send_sem=ss,
            recv_sem=rs,
            device_id=(gx, gy, beyond),
            device_id_type=MESH,
        )

    sub = lax.broadcasted_iota(jnp.int32, (8, 128), 0)
    lane = lax.broadcasted_iota(jnp.int32, (8, 128), 1)
    matched = ((sub < 6) & (lane // 32 == sub % 3)) | ((sub >= 6) & (lane >= 96))
    slot_of = jnp.where(sub < 6, sub // 3, sub - 6)
    index = lane % 32

    cell = jnp.zeros((8, 128), jnp.int32)
    for b in range(32):
        cell = jnp.where(index == b, cells[b], cell)
    width = 8 * n_gy

    def source_of(c):
        column = c // 2
        return (column // width) // 4 * n_gy + (column % width) // 8

    source = source_of(cell)
    local = (cell // 2 // width) % 4 * 8 + (cell // 2 % width) % 8
    rank = jnp.zeros((8, 128), jnp.int32)
    for b in range(31):
        rank = rank + jnp.where((source == source_of(cells[b])) & (index > b), 1, 0)
    code = jnp.where(matched, 2 * source + rank - slot_of, -1000000)
    target = lax.broadcasted_iota(jnp.int32, (devices, 8, 128), 0) * 2
    hot = jnp.where(code[None] == target, 1.0, 0.0).astype(F32).reshape(devices * 8, 128)
    pick_h[:, 0:128] = hot.astype(BF16)
    pick_h[:, 128:256] = hot.astype(BF16)
    pick_ht[...] = hot.T.astype(BF16)

    def spread(pick, table):
        high, low = split(table)
        both = jnp.concatenate([high, low], axis=0)
        rows = jnp.dot(pick[...], both, preferred_element_type=F32)
        return rows.reshape(devices, 8, 128)

    def collect(pick_t, tiles, masked):
        rows = tiles.reshape(devices * 8, 128)
        if masked:
            inside = lax.broadcasted_iota(jnp.int32, (devices * 8, 128), 0) % 8 < 6
            rows = jnp.where(inside, rows, 0.0)
        high, low = split(rows)
        table = pick_t[...]
        return jnp.dot(table, high, preferred_element_type=F32) + jnp.dot(
            table, low, preferred_element_type=F32
        )

    column = lax.broadcasted_iota(jnp.int32, (128, 128), 0)
    lanes = lax.broadcasted_iota(jnp.int32, (128, 128), 1)
    own = jnp.where(column % 32 == lanes, jnp.broadcast_to(local[0:1] + 1, (128, 128)), 0)
    ids = jnp.sum(own.astype(F32), axis=1, keepdims=True)
    ids = jnp.where(column >= 96, jnp.broadcast_to(ids, (128, 128)), 0.0)
    id_out[...] = spread(pick_h, ids)

    live = slots[...].astype(F32)
    rate = drag_factor * vol[...] * live
    links = contacts[...].astype(F32).astype(BF16)
    count = jnp.dot(links, live.astype(BF16), preferred_element_type=F32)

    def weighted(v):
        return jnp.concatenate([rate * v[0], rate * v[1], rate * v[2], rate], axis=0)

    def near(moving):
        high, low = split(moving)
        return jnp.dot(links, high, preferred_element_type=F32) + jnp.dot(
            links, low, preferred_element_type=F32
        )

    velocity = [vel[a] for a in range(3)]
    w_out[0] = spread(pick_h, weighted(velocity))

    def moments(read):
        rho = jnp.zeros((32, 128), F32)
        momentum = [jnp.zeros((32, 128), F32) for _ in range(3)]
        for i in range(19):
            f = read(i)
            rho = rho + f
            for a in range(3):
                if VELOCITIES[i][a] == 1:
                    momentum[a] = momentum[a] + f
                elif VELOCITIES[i][a] == -1:
                    momentum[a] = momentum[a] - f
        return rho, [m / rho for m in momentum]

    def flow_rows(u):
        return jnp.concatenate([u[0], u[1], u[2], jnp.zeros((32, 128), F32)], axis=0)

    read_first = lambda i: pop[i].reshape(32, 128)
    read_next = lambda i: fnow[pl.ds(i * 32, 32), :]
    flow = moments(read_first)

    pl.semaphore_wait(barrier, devices - 1 + len(across))
    exchange(id_out, id_in, 6, 2, id_ss, id_rs)
    exchange(w_out.at[0], w_in.at[0], 0, 8, w_ss.at[0], w_rs.at[0])

    id_wait = whole(id_out, id_in, 6, 2, id_ss, id_rs)
    id_wait.wait_recv()
    first = jnp.broadcast_to(id_in[:, 6:7, :], (devices, 8, 128))
    second = jnp.broadcast_to(id_in[:, 7:8, :], (devices, 8, 128))
    held = jnp.where((slot_of == 0)[None], first, second)
    wanted = jnp.where(matched, index + 1, -1).astype(F32)
    hot_c = jnp.where(held == wanted[None], 1.0, 0.0).astype(F32).reshape(devices * 8, 128)
    pick_c[:, 0:128] = hot_c.astype(BF16)
    pick_c[:, 128:256] = hot_c.astype(BF16)

    def send_flow(t, u):
        u_out[t] = spread(pick_c, flow_rows(u))
        exchange(u_out.at[t], u_in.at[t], 0, 6, u_ss.at[t], u_rs.at[t])

    def wait_flow(t):
        whole(u_out.at[t], u_in.at[t], 0, 6, u_ss.at[t], u_rs.at[t]).wait_recv()

    def w_rows(t):
        return 8 if t == 0 else 6

    def send_weight(t, v):
        w_out[t] = spread(pick_h, weighted(v))
        exchange(w_out.at[t], w_in.at[t], 0, w_rows(t), w_ss.at[t], w_rs.at[t])

    def wait_weight(t):
        whole(w_out.at[t], w_in.at[t], 0, w_rows(t), w_ss.at[t], w_rs.at[t]).wait_recv()

    def advance(t, v):
        wait_flow(t)
        block = collect(pick_ht, u_in[t], True)
        updated = []
        for a in range(3):
            u = block[a * 32 : a * 32 + 32]
            drag = rate * (u - v[a])
            push = contact_stiffness * live * (near(v[a] * live) - count * v[a])
            value = v[a] + drag + push
            if a == 2:
                value = value - gravity * live
            updated.append(value)
        return updated

    def halo_copy(t, first_out, tiles, first_in, px, py, pz):
        return pltpu.make_async_remote_copy(
            src_ref=halo_out.at[t, pl.ds(first_out, tiles)],
            dst_ref=halo_in.at[t, pl.ds(first_in, tiles)],
            send_sem=h_ss.at[t],
            recv_sem=h_rs.at[t],
            device_id=(px, py, pz),
            device_id_type=MESH,
        )

    def collide(t, read, flow, field):
        rho, speed = flow
        scale = 1.0 / (1.0 + 0.5 * field[3])
        force = [field[a] - field[3] * speed[a] for a in range(3)]
        target = [scale * (speed[a] + relax_time * force[a] / rho) for a in range(3)]
        square = target[0] * target[0] + target[1] * target[1] + target[2] * target[2]
        base = 1.0 - 1.5 * square
        for i in range(19):
            along = None
            for a in range(3):
                c = VELOCITIES[i][a]
                if c == 1:
                    along = target[a] if along is None else along + target[a]
                elif c == -1:
                    along = -target[a] if along is None else along - target[a]
            shape = base if along is None else base + along * (3.0 + 4.5 * along)
            f = read(i)
            post[pl.ds(i * 32, 32), :] = f - (f - WEIGHTS[i] * rho * shape) / relax_time

    def tile(i, x):
        return post[pl.ds(i * 32 + x * 8, 8), :]

    def send_halo(t):
        for n in range(5):
            halo_out[t, n] = tile(X_UP[n], 3)
            halo_out[t, 5 + n] = tile(X_DOWN[n], 0)
            half = pl.ds((n % 2) * 4, 4)
            halo_out[t, 10 + n // 2, half, :] = post[pl.ds(Y_UP[n] * 32 + 7, 4, stride=8), :]
            halo_out[t, 13 + n // 2, half, :] = post[pl.ds(Y_DOWN[n] * 32, 4, stride=8), :]
        halo_out[t, 12, 4:8, :] = jnp.zeros((4, 128), F32)
        halo_out[t, 15, 4:8, :] = jnp.zeros((4, 128), F32)
        packed = jnp.zeros((8, 128), F32)
        for n in range(5):
            for x in range(4):
                k = n * 4 + x
                up = pltpu.roll(tile(Z_UP[n], x), (k + 1) % 128, 1)
                down = pltpu.roll(tile(Z_DOWN[n], x), k, 1) if k else tile(Z_DOWN[n], x)
                packed = jnp.where(lane == k, jnp.where(gz == 0, up, down), packed)
        halo_out[t, 16] = packed
        halo_copy(t, 0, 5, 0, east, gy, gz).start()
        halo_copy(t, 5, 5, 5, west, gy, gz).start()
        halo_copy(t, 10, 3, 10, gx, north, gz).start()
        halo_copy(t, 13, 3, 13, gx, south, gz).start()
        halo_copy(t, 1, 1, 16, east, north, gz).start()
        halo_copy(t, 6, 1, 17, west, south, gz).start()
        halo_copy(t, 2, 1, 18, east, south, gz).start()
        halo_copy(t, 7, 1, 19, west, north, gz).start()
        for n, (px, py) in enumerate(across):
            halo_copy(t, 16, 1, 20 + n, px, py, beyond).start()

    def halo_whole(t):
        return pltpu.make_async_remote_copy(
            src_ref=halo_in.at[t],
            dst_ref=halo_in.at[t],
            send_sem=h_ss.at[t],
            recv_sem=h_rs.at[t],
            device_id=(gx, gy, beyond),
            device_id_type=MESH,
        )

    def stream(t, write):
        halo_whole(t).wait_recv()
        level = halo_in[t, 20]
        block_of = lane // 4
        from_west = pltpu.roll(halo_in[t, 21], 125, 1)
        from_east = pltpu.roll(halo_in[t, 22], 3, 1)
        right = jnp.where(lane % 4 == 0, from_west, pltpu.roll(level, 1, 1))
        left = jnp.where(lane % 4 == 3, from_east, pltpu.roll(level, 127, 1))
        upper = jnp.where(sub == 0, pltpu.roll(halo_in[t, 23], 1, 0), pltpu.roll(level, 1, 0))
        lower = jnp.where(sub == 7, pltpu.roll(halo_in[t, 24], 7, 0), pltpu.roll(level, 7, 0))
        ghost = jnp.where(block_of == 1, right, level)
        ghost = jnp.where(block_of == 2, left, ghost)
        ghost = jnp.where(block_of == 3, upper, ghost)
        ghost = jnp.where(block_of == 4, lower, ghost)

        for i in range(19):
            cx, cy, cz = VELOCITIES[i]
            for x in range(4):
                sx = x - cx
                inside = 0 <= sx < 4
                if inside:
                    value = tile(i, sx)
                elif cx == 1:
                    value = halo_in[t, X_UP.index(i)]
                else:
                    value = halo_in[t, 5 + X_DOWN.index(i)]
                if cy == 1:
                    n = Y_UP.index(i)
                    if inside:
                        row = jnp.broadcast_to(
                            halo_in[t, 10 + n // 2, pl.ds((n % 2) * 4 + sx, 1), :], (8, 128)
                        )
                    else:
                        row = jnp.broadcast_to(
                            halo_in[t, 16 if cx == 1 else 19, pl.ds(7, 1), :], (8, 128)
                        )
                    value = jnp.where(sub == 0, row, pltpu.roll(value, 1, 0))
                elif cy == -1:
                    n = Y_DOWN.index(i)
                    if inside:
                        row = jnp.broadcast_to(
                            halo_in[t, 13 + n // 2, pl.ds((n % 2) * 4 + sx, 1), :], (8, 128)
                        )
                    else:
                        row = jnp.broadcast_to(
                            halo_in[t, 18 if cx == 1 else 17, pl.ds(0, 1), :], (8, 128)
                        )
                    value = jnp.where(sub == 7, row, pltpu.roll(value, 7, 0))
                if cz != 0:
                    n = (Z_UP if cz == 1 else Z_DOWN).index(i)
                    k = n * 4 + x
                    edge = jnp.broadcast_to(ghost[:, k : k + 1], (8, 128))
                    wall = tile(OPPOSITE[i], x)
                    if cz == 1:
                        edge = jnp.where(gz == 1, edge, wall)
                        value = jnp.where(lane == 0, edge, pltpu.roll(value, 1, 1))
                    else:
                        edge = jnp.where(gz == 0, edge, wall)
                        value = jnp.where(lane == 127, edge, pltpu.roll(value, 127, 1))
                write(i, x, value)

    def write_next(i, x, value):
        fnow[pl.ds(i * 32 + x * 8, 8), :] = value

    def write_last(i, x, value):
        fluid[i, x] = value

    solid = None

    def fluid_step(t, read, flow, write):
        nonlocal solid
        wait_weight(t)
        table = collect(pick_ct, w_in[t], t > 0)
        if t == 0:
            solid = table[96:128]
        field = [table[a * 32 : a * 32 + 32] for a in range(3)] + [solid]
        collide(t, read, flow, field)
        send_halo(t)
        stream(t, write)

    send_flow(0, flow[1])
    pick_ct[...] = hot_c.T.astype(BF16)
    fluid_step(0, read_first, flow, write_next)
    flow = moments(read_next)
    send_flow(1, flow[1])
    velocity = advance(0, velocity)
    send_weight(1, velocity)
    velocity = advance(1, velocity)
    send_weight(2, velocity)
    fluid_step(1, read_next, flow, write_next)
    flow = moments(read_next)
    send_flow(2, flow[1])
    fluid_step(2, read_next, flow, write_next)
    flow = moments(read_next)
    send_flow(3, flow[1])
    velocity = advance(2, velocity)
    send_weight(3, velocity)
    velocity = advance(3, velocity)
    for a in range(3):
        grains[a] = velocity[a]
    fluid_step(3, read_next, flow, write_last)

    id_wait.wait_send()
    for t in range(SUBSTEPS):
        whole(u_out.at[t], u_in.at[t], 0, 6, u_ss.at[t], u_rs.at[t]).wait_send()
        whole(w_out.at[t], w_in.at[t], 0, w_rows(t), w_ss.at[t], w_rs.at[t]).wait_send()
        halo_whole(t).wait_send()


def solution(mesh):
    n_gx, n_gy = mesh.shape["gx"], mesh.shape["gy"]
    devices = n_gx * n_gy
    vmem = pl.BlockSpec(memory_space=pltpu.VMEM)
    smem = pl.BlockSpec(memory_space=pltpu.SMEM)
    dma = pltpu.SemaphoreType.DMA

    def body(populations, grain_velocity, grain_volume, slots, contacts, bin_cell):
        return pl.pallas_call(
            lambda *refs: kernel(n_gx, n_gy, *refs),
            out_shape=(
                jax.ShapeDtypeStruct(populations.shape, F32),
                jax.ShapeDtypeStruct(grain_velocity.shape, F32),
            ),
            in_specs=[vmem] * 5 + [smem],
            out_specs=(vmem, vmem),
            scratch_shapes=[
                pltpu.VMEM((608, 128), F32),
                pltpu.VMEM((608, 128), F32),
                pltpu.VMEM((devices * 8, 256), BF16),
                pltpu.VMEM((128, devices * 8), BF16),
                pltpu.VMEM((devices * 8, 256), BF16),
                pltpu.VMEM((128, devices * 8), BF16),
                pltpu.VMEM((devices, 8, 128), F32),
                pltpu.VMEM((devices, 8, 128), F32),
                pltpu.VMEM((SUBSTEPS, devices, 8, 128), F32),
                pltpu.VMEM((SUBSTEPS, devices, 8, 128), F32),
                pltpu.VMEM((SUBSTEPS, devices, 8, 128), F32),
                pltpu.VMEM((SUBSTEPS, devices, 8, 128), F32),
                pltpu.VMEM((SUBSTEPS, 17, 8, 128), F32),
                pltpu.VMEM((SUBSTEPS, 25, 8, 128), F32),
                dma,
                dma,
                dma((SUBSTEPS,)),
                dma((SUBSTEPS,)),
                dma((SUBSTEPS,)),
                dma((SUBSTEPS,)),
                dma((SUBSTEPS,)),
                dma((SUBSTEPS,)),
            ],
            compiler_params=pltpu.CompilerParams(
                collective_id=0, has_side_effects=True, vmem_limit_bytes=48 << 20
            ),
            name="bed",
        )(populations, grain_velocity, grain_volume, slots, contacts, bin_cell)

    every = ("gx", "gy", "gz")
    in_specs = (
        P(None, "gx", "gy", "gz"),
        P(None, every, None),
        P(every, None),
        P(every, None),
        P(every, None),
        P(every),
    )
    out_specs = (P(None, "gx", "gy", "gz"), P(None, every, None))
    return jax.shard_map(body, mesh=mesh, in_specs=in_specs, out_specs=out_specs, check_vma=False)
```

profile of v0, /device:TPU:1, one launch (start us, length us, event | category | flops | bytes accessed | tf_op | source)
XLA Modules:
  0.0 115.7 jit_solution(2709543606147174494)
XLA Ops:
  0.6 0.0 copy-start
  0.6 1.0 copy-done
  1.6 0.0 copy-start.1
  1.6 0.8 copy-done.1
  2.4 0.0 copy-start.2
  2.4 0.7 copy-done.2
  3.1 0.0 copy-start.3
  3.1 0.7 copy-done.3
  3.8 0.0 copy-start.4
  3.8 0.7 copy-done.4
  4.6 0.0 copy-start.5
  4.6 0.7 copy-done.5
  5.2 109.1 %bed.1 = (f32[19,4,8,128]{3,2,1,0:T(8,128)S(1)}, f32[3,32,128]{2,1,0:T(8,128)S(1)}) custom-call(f32[19,4,8,128]{3,2,1,0:T(8,128)S(1)} %copy-done, f32[3,32,128]{2,1,0:T(8,128)S(1)} %copy-done.1, f32[32,128]{1,0:T(8,128)S(1)} %copy-done.2, s32[32,128]{1,0:T(8,128)S(1)} %copy-done.3, s32[32,32]{1,0:T(8,128)S(1)} %copy-done.4, s32[32]{0:T(128)S(1)} %copy-done.5), custom_call_target="tpu_custom_call" | custom-call | tf_op jit(solution)/shard_map/bed/pallas_call | solution.py:443
  114.3 0.7 copy.10
  115.1 0.6 copy.11
Async XLA Ops:
  0.6 1.0 copy-start
  1.6 0.8 copy-start.1
  2.4 0.7 copy-start.2
  3.1 0.7 copy-start.3
  3.8 0.7 copy-start.4
  4.6 0.7 copy-start.5
where the time goes:
time: 116 us
  Pallas kernels  109 us (94%)
  local copies, waits for them, and re-layouts  5.9 us (5%)
    pallas_call x1, Pallas kernels, body(): pl.pallas_call(lambda *refs: kernel(n_gx, n_gy, *refs), out_shape=(jax.Sh...  109 us
    unnamed x14, local copies, waits for them, and re-layouts  5.9 us

commit v1 on v0

--- a/solution.py
+++ b/solution.py
@@ -179,6 +179,16 @@
     def weighted(v):
         return jnp.concatenate([rate * v[0], rate * v[1], rate * v[2], rate], axis=0)
 
+    def contact_push(v):
+        pushed = []
+        for a in range(3):
+            push = contact_stiffness * live * (near(v[a] * live) - count * v[a])
+            pushed.append(push - gravity * live if a == 2 else push)
+        return pushed
+
+    def without_flow(v, pushed):
+        return [(1.0 - rate) * v[a] + pushed[a] for a in range(3)]
+
     def near(moving):
         high, low = split(moving)
         return jnp.dot(links, high, preferred_element_type=F32) + jnp.dot(
@@ -210,7 +220,10 @@
 
     pl.semaphore_wait(barrier, devices - 1 + len(across))
     exchange(id_out, id_in, 6, 2, id_ss, id_rs)
-    exchange(w_out.at[0], w_in.at[0], 0, 8, w_ss.at[0], w_rs.at[0])
+    def w_rows(t):
+        return 8 if t == 0 else 6
+
+    exchange(w_out.at[0], w_in.at[0], 0, w_rows(0), w_ss.at[0], w_rs.at[0])
 
     id_wait = whole(id_out, id_in, 6, 2, id_ss, id_rs)
     id_wait.wait_recv()
@@ -229,8 +242,6 @@
     def wait_flow(t):
         whole(u_out.at[t], u_in.at[t], 0, 6, u_ss.at[t], u_rs.at[t]).wait_recv()
 
-    def w_rows(t):
-        return 8 if t == 0 else 6
 
     def send_weight(t, v):
         w_out[t] = spread(pick_h, weighted(v))
@@ -239,18 +250,13 @@
     def wait_weight(t):
         whole(w_out.at[t], w_in.at[t], 0, w_rows(t), w_ss.at[t], w_rs.at[t]).wait_recv()
 
-    def advance(t, v):
+    def advance(t, v, pushed):
         wait_flow(t)
         block = collect(pick_ht, u_in[t], True)
         updated = []
         for a in range(3):
             u = block[a * 32 : a * 32 + 32]
-            drag = rate * (u - v[a])
-            push = contact_stiffness * live * (near(v[a] * live) - count * v[a])
-            value = v[a] + drag + push
-            if a == 2:
-                value = value - gravity * live
-            updated.append(value)
+            updated.append(v[a] + rate * (u - v[a]) + pushed[a])
         return updated
 
     def halo_copy(t, first_out, tiles, first_in, px, py, pz):
@@ -390,40 +396,62 @@
     def write_last(i, x, value):
         fluid[i, x] = value
 
-    solid = None
-
-    def fluid_step(t, read, flow, write):
-        nonlocal solid
-        wait_weight(t)
-        table = collect(pick_ct, w_in[t], t > 0)
-        if t == 0:
-            solid = table[96:128]
-        field = [table[a * 32 : a * 32 + 32] for a in range(3)] + [solid]
+    def fluid_step(t, read, flow, field, write):
         collide(t, read, flow, field)
         send_halo(t)
         stream(t, write)
 
+    def field_of(t, before):
+        wait_weight(t)
+        table = collect(pick_ct, w_in[t], True)
+        parts = [table[a * 32 : a * 32 + 32] + solid2 * before[a] for a in range(3)]
+        return parts + [solid]
+
     send_flow(0, flow[1])
+    pushed = contact_push(velocity)
+    send_weight(1, without_flow(velocity, pushed))
     pick_ct[...] = hot_c.T.astype(BF16)
-    fluid_step(0, read_first, flow, write_next)
+
+    wait_weight(0)
+    table = collect(pick_ct, w_in[0], False)
+    solid = table[96:128]
+    field = [table[a * 32 : a * 32 + 32] for a in range(3)] + [solid]
+    collide(0, read_first, flow, field)
+    send_halo(0)
+    tail = w_in[0].reshape(devices * 8, 128)
+    tail = jnp.where(lax.broadcasted_iota(jnp.int32, (devices * 8, 128), 0) % 8 < 6, 0.0, tail)
+    solid2 = collect(pick_ct, tail * tail, False)[96:128]
+    stream(0, write_next)
+    before = flow[1]
     flow = moments(read_next)
     send_flow(1, flow[1])
-    velocity = advance(0, velocity)
-    send_weight(1, velocity)
-    velocity = advance(1, velocity)
-    send_weight(2, velocity)
-    fluid_step(1, read_next, flow, write_next)
+
+    velocity = advance(0, velocity, pushed)
+    pushed = contact_push(velocity)
+    send_weight(2, without_flow(velocity, pushed))
+
+    fluid_step(1, read_next, flow, field_of(1, before), write_next)
+    before = flow[1]
     flow = moments(read_next)
     send_flow(2, flow[1])
-    fluid_step(2, read_next, flow, write_next)
+
+    velocity = advance(1, velocity, pushed)
+    pushed = contact_push(velocity)
+    send_weight(3, without_flow(velocity, pushed))
+
+    fluid_step(2, read_next, flow, field_of(2, before), write_next)
+    before = flow[1]
     flow = moments(read_next)
     send_flow(3, flow[1])
-    velocity = advance(2, velocity)
-    send_weight(3, velocity)
-    velocity = advance(3, velocity)
+
+    velocity = advance(2, velocity, pushed)
+    pushed = contact_push(velocity)
+
+    fluid_step(3, read_next, flow, field_of(3, before), write_last)
+
+    velocity = advance(3, velocity, pushed)
     for a in range(3):
         grains[a] = velocity[a]
-    fluid_step(3, read_next, flow, write_last)
 
     id_wait.wait_send()
     for t in range(SUBSTEPS):

time: 116 us -> 112 us (0.966)
  Pallas kernels: 109 us -> 105 us
    pallas_call x1, Pallas kernels: 109 us -> 105 us  [body(): pl.pallas_call(lambda *refs: kernel(n_gx, n_gy, *refs), out_shape=(jax.Sh...]
where the time goes in v1:
time: 112 us
  Pallas kernels  105 us (94%)
  local copies, waits for them, and re-layouts  5.9 us (5%)
    pallas_call x1, Pallas kernels, body(): pl.pallas_call(lambda *refs: kernel(n_gx, n_gy, *refs), out_shape=(jax.Sh...  105 us
    unnamed x14, local copies, waits for them, and re-layouts  5.9 us

profile of v1, /device:TPU:1, one launch (start us, length us, event | category | flops | bytes accessed | tf_op | source)
XLA Modules:
  0.0 111.6 jit_solution(12643509427906492215)
XLA Ops:
  0.6 0.0 copy-start
  0.6 1.0 copy-done
  1.6 0.0 copy-start.1
  1.6 0.8 copy-done.1
  2.4 0.0 copy-start.2
  2.4 0.7 copy-done.2
  3.1 0.0 copy-start.3
  3.1 0.7 copy-done.3
  3.8 0.0 copy-start.4
  3.8 0.7 copy-done.4
  4.6 0.0 copy-start.5
  4.6 0.7 copy-done.5
  5.2 105.0 %bed.1 = (f32[19,4,8,128]{3,2,1,0:T(8,128)S(1)}, f32[3,32,128]{2,1,0:T(8,128)S(1)}) custom-call(f32[19,4,8,128]{3,2,1,0:T(8,128)S(1)} %copy-done, f32[3,32,128]{2,1,0:T(8,128)S(1)} %copy-done.1, f32[32,128]{1,0:T(8,128)S(1)} %copy-done.2, s32[32,128]{1,0:T(8,128)S(1)} %copy-done.3, s32[32,32]{1,0:T(8,128)S(1)} %copy-done.4, s32[32]{0:T(128)S(1)} %copy-done.5), custom_call_target="tpu_custom_call" | custom-call | tf_op jit(solution)/shard_map/bed/pallas_call | solution.py:471
  110.3 0.7 copy.10
  111.0 0.6 copy.11
Async XLA Ops:
  0.6 1.0 copy-start
  1.6 0.8 copy-start.1
  2.4 0.7 copy-start.2
  3.1 0.7 copy-start.3
  3.8 0.7 copy-start.4
  4.6 0.7 copy-start.5

commit v2 on v1

--- a/solution.py
+++ b/solution.py
@@ -27,6 +27,8 @@
 Y_DOWN = [4, 8, 9, 16, 18]
 Z_UP = [5, 11, 14, 15, 18]
 Z_DOWN = [6, 13, 12, 17, 16]
+SOURCE = [0, -1, 1, -2, 2, -3, 3, 4]
+GROUPS = [(0, 1), (1, 4), (5, 3)]
 
 F32 = jnp.float32
 BF16 = jnp.bfloat16
@@ -43,74 +45,74 @@
     n_gx, n_gy,
     pop, vel, vol, slots, contacts, cells,
     fluid, grains,
-    post, fnow, pick_h, pick_ht, pick_c, pick_ct,
-    id_out, id_in, u_out, u_in, w_out, w_in, halo_out, halo_in,
-    id_ss, id_rs, u_ss, u_rs, w_ss, w_rs, h_ss, h_rs,
+    post, fnow, pick_w, pick_u, pick_ht, pick_ct,
+    idh_out, idh_in, idw_out, idw_in,
+    u_raw, w_raw, u_out, u_in, w_out, w_in, halo_out, halo_in,
+    idh_ss, idh_rs, idw_ss, idw_rs,
+    u_zss, u_zrs, u_ss, u_rs, w_zss, w_zrs, w_ss, w_rs, h_ss, h_rs,
 ):
-    devices = n_gx * n_gy
-    n_xh, n_z, n_y, n_c = 2, n_gx // 2, n_gy // 2, 2
+    n_z, n_c = 8, 2
+    n_xh, n_y = n_gx // n_z, n_gy // n_c
+    plane = n_xh * n_gy
     gx, gy, gz = lax.axis_index("gx"), lax.axis_index("gy"), lax.axis_index("gz")
-    me = gx * n_gy + gy
     xh, zc, yc, cc = gx // n_z, gx % n_z, gy // n_c, gy % n_c
-    far = n_z // 2
-    z_order = []
-    for s in range(far, -1, -1):
-        for d in (s, (n_z - s) % n_z):
-            if d not in z_order:
-                z_order.append(d)
-
-    def to_all(act):
-        groups = n_xh * n_y * n_c
-
-        def dest(m, dz):
-            px = (xh + m // (n_y * n_c)) % n_xh
-            py = (yc + (m // n_c) % n_y) % n_y
-            pc = (cc + m % n_c) % n_c
-            pz = (zc + dz) % n_z
-            return px * n_z + pz, py * n_c + pc
-
-        def group(i, carry):
-            for dz in z_order:
-                act(*dest(groups - 1 - i, dz))
-            return carry
-
-        lax.fori_loop(0, groups - 1, group, 0)
-        for dz in z_order:
-            if dz != 0:
-                act(*dest(0, dz))
+    me = xh * n_gy + gy
+
+    def along_z(by):
+        return (xh * n_z + (zc + by + n_z) % n_z, gy, gz)
+
+    def in_plane(m):
+        px = (xh + m // n_gy) % n_xh
+        py = (yc + (m // n_c) % n_y) % n_y * n_c + (cc + m % n_c) % n_c
+        return px, py
 
     west, east = (gx + n_gx - 1) % n_gx, (gx + 1) % n_gx
     south, north = (gy + n_gy - 1) % n_gy, (gy + 1) % n_gy
     beyond = 1 - gz
     across = [(gx, gy), (east, gy), (west, gy), (gx, north), (gx, south)]
+    corners = [(east, north), (west, south), (east, south), (west, north)]
 
     barrier = pltpu.get_barrier_semaphore()
-
-    def greet(px, py):
-        pl.semaphore_signal(barrier, inc=1, device_id=(px, py, gz), device_id_type=MESH)
-
-    to_all(greet)
-    for px, py in across:
-        pl.semaphore_signal(barrier, inc=1, device_id=(px, py, beyond), device_id_type=MESH)
-
-    def exchange(out, inn, row, rows, ss, rs):
-        here = pl.ds(row, rows)
-
-        def copy(px, py):
+    greeted = [along_z(by) for by in (2, -2, 1, -1)]
+    for m in range(plane - 1, 0, -1):
+        px, py = in_plane(m)
+        greeted.append((px * n_z + zc, py, gz))
+    greeted += [(px, py, gz) for px, py in [(east, gy), (west, gy)] + corners]
+    greeted += [(px, py, beyond) for px, py in across]
+    for device in greeted:
+        pl.semaphore_signal(barrier, inc=1, device_id=device, device_id_type=MESH)
+
+    def z_copy(raw, t, source, region, by, start, rows, ss, rs, sem):
+        part = pl.ds(start, rows)
+        return pltpu.make_async_remote_copy(
+            src_ref=raw.at[t, source, part],
+            dst_ref=raw.at[t, region, part],
+            send_sem=ss.at[t],
+            recv_sem=rs.at[t, sem],
+            device_id=along_z(by),
+            device_id_type=MESH,
+        )
+
+    def plane_send(out, inn, ss, rs, first, tiles, row, rows):
+        part = (pl.ds(first, tiles), pl.ds(row, rows))
+
+        def send(i, carry):
+            px, py = in_plane(plane - 1 - i)
             pltpu.make_async_remote_copy(
-                src_ref=out.at[px * n_gy + py, here],
-                dst_ref=inn.at[me, here],
+                src_ref=out.at[(px * n_gy + py,) + part],
+                dst_ref=inn.at[(me,) + part],
                 send_sem=ss,
                 recv_sem=rs,
-                device_id=(px, py, gz),
+                device_id=(px * n_z + zc, py, gz),
                 device_id_type=MESH,
             ).start()
-
-        to_all(copy)
-        inn[me] = out[me]
-
-    def whole(out, inn, row, rows, ss, rs):
-        span = (pl.ds(0, devices - 1), pl.ds(row, rows))
+            return carry
+
+        lax.fori_loop(0, plane - 1, send, 0)
+        inn[me, pl.ds(first, tiles)] = out[me, pl.ds(first, tiles)]
+
+    def plane_whole(out, inn, ss, rs, first, tiles, row, rows):
+        span = (pl.ds(0, plane - 1), pl.ds(first, tiles), pl.ds(row, rows))
         return pltpu.make_async_remote_copy(
             src_ref=out.at[span],
             dst_ref=inn.at[span],
@@ -140,23 +142,38 @@
     rank = jnp.zeros((8, 128), jnp.int32)
     for b in range(31):
         rank = rank + jnp.where((source == source_of(cells[b])) & (index > b), 1, 0)
-    code = jnp.where(matched, 2 * source + rank - slot_of, -1000000)
-    target = lax.broadcasted_iota(jnp.int32, (devices, 8, 128), 0) * 2
-    hot = jnp.where(code[None] == target, 1.0, 0.0).astype(F32).reshape(devices * 8, 128)
-    pick_h[:, 0:128] = hot.astype(BF16)
-    pick_h[:, 128:256] = hot.astype(BF16)
-    pick_ht[...] = hot.T.astype(BF16)
+
+    def placed(device):
+        x, y = device // n_gy, device % n_gy
+        return x // n_z * n_gy + y, x % n_z
+
+    def hot_ids(hot, column):
+        return jnp.sum(hot * column, axis=-1, keepdims=True)
+
+    side, depth = placed(source)
+    away = (depth - zc + n_z) % n_z
+    region_of = jnp.zeros((8, 128), jnp.int32)
+    for r, by in enumerate(SOURCE):
+        region_of = jnp.where(away == by % n_z, r, region_of)
+    code = jnp.where(matched, 2 * (side * n_z + region_of) + rank - slot_of, -1000000)
+    target = lax.broadcasted_iota(jnp.int32, (plane * n_z, 8, 128), 0) * 2
+    hot_h = jnp.where(code[None] == target, 1.0, 0.0).astype(F32)
+    column = (local + 1).astype(F32)
+    idh_out[...] = jnp.broadcast_to(
+        hot_ids(hot_h, column[None]), (plane * n_z, 8, 128)
+    ).reshape(plane, n_z, 8, 128)
 
     def spread(pick, table):
+        if table.shape[0] == 96:
+            table = jnp.concatenate([table, jnp.zeros((32, 128), F32)], axis=0)
         high, low = split(table)
         both = jnp.concatenate([high, low], axis=0)
-        rows = jnp.dot(pick[...], both, preferred_element_type=F32)
-        return rows.reshape(devices, 8, 128)
-
-    def collect(pick_t, tiles, masked):
-        rows = tiles.reshape(devices * 8, 128)
+        rows = jnp.dot(pick, both, preferred_element_type=F32)
+        return rows.reshape(plane, 8, 128)
+
+    def collect(pick_t, rows, masked):
         if masked:
-            inside = lax.broadcasted_iota(jnp.int32, (devices * 8, 128), 0) % 8 < 6
+            inside = lax.broadcasted_iota(jnp.int32, rows.shape, 0) % 8 < 6
             rows = jnp.where(inside, rows, 0.0)
         high, low = split(rows)
         table = pick_t[...]
@@ -164,20 +181,19 @@
             table, low, preferred_element_type=F32
         )
 
-    column = lax.broadcasted_iota(jnp.int32, (128, 128), 0)
-    lanes = lax.broadcasted_iota(jnp.int32, (128, 128), 1)
-    own = jnp.where(column % 32 == lanes, jnp.broadcast_to(local[0:1] + 1, (128, 128)), 0)
-    ids = jnp.sum(own.astype(F32), axis=1, keepdims=True)
-    ids = jnp.where(column >= 96, jnp.broadcast_to(ids, (128, 128)), 0.0)
-    id_out[...] = spread(pick_h, ids)
+    def flat(tiles):
+        return tiles.reshape(plane * n_z * 8, 128)
 
     live = slots[...].astype(F32)
     rate = drag_factor * vol[...] * live
     links = contacts[...].astype(F32).astype(BF16)
     count = jnp.dot(links, live.astype(BF16), preferred_element_type=F32)
 
-    def weighted(v):
-        return jnp.concatenate([rate * v[0], rate * v[1], rate * v[2], rate], axis=0)
+    def near(moving):
+        high, low = split(moving)
+        return jnp.dot(links, high, preferred_element_type=F32) + jnp.dot(
+            links, low, preferred_element_type=F32
+        )
 
     def contact_push(v):
         pushed = []
@@ -186,17 +202,11 @@
             pushed.append(push - gravity * live if a == 2 else push)
         return pushed
 
-    def without_flow(v, pushed):
-        return [(1.0 - rate) * v[a] + pushed[a] for a in range(3)]
-
-    def near(moving):
-        high, low = split(moving)
-        return jnp.dot(links, high, preferred_element_type=F32) + jnp.dot(
-            links, low, preferred_element_type=F32
-        )
-
     velocity = [vel[a] for a in range(3)]
-    w_out[0] = spread(pick_h, weighted(velocity))
+    for a in range(3):
+        w_raw[0, 0, a * 32 : a * 32 + 32, :] = rate * velocity[a]
+    w_raw[0, 0, 96:128, :] = rate
+    w_raw[0, 0, 128:136, :] = jnp.where(sub == 0, 2 * source + rank, local + 1).astype(F32)
 
     def moments(read):
         rho = jnp.zeros((32, 128), F32)
@@ -211,48 +221,138 @@
                     momentum[a] = momentum[a] - f
         return rho, [m / rho for m in momentum]
 
-    def flow_rows(u):
-        return jnp.concatenate([u[0], u[1], u[2], jnp.zeros((32, 128), F32)], axis=0)
-
     read_first = lambda i: pop[i].reshape(32, 128)
     read_next = lambda i: fnow[pl.ds(i * 32, 32), :]
     flow = moments(read_first)
 
-    pl.semaphore_wait(barrier, devices - 1 + len(across))
-    exchange(id_out, id_in, 6, 2, id_ss, id_rs)
-    def w_rows(t):
-        return 8 if t == 0 else 6
-
-    exchange(w_out.at[0], w_in.at[0], 0, w_rows(0), w_ss.at[0], w_rs.at[0])
-
-    id_wait = whole(id_out, id_in, 6, 2, id_ss, id_rs)
-    id_wait.wait_recv()
-    first = jnp.broadcast_to(id_in[:, 6:7, :], (devices, 8, 128))
-    second = jnp.broadcast_to(id_in[:, 7:8, :], (devices, 8, 128))
-    held = jnp.where((slot_of == 0)[None], first, second)
-    wanted = jnp.where(matched, index + 1, -1).astype(F32)
-    hot_c = jnp.where(held == wanted[None], 1.0, 0.0).astype(F32).reshape(devices * 8, 128)
-    pick_c[:, 0:128] = hot_c.astype(BF16)
-    pick_c[:, 128:256] = hot_c.astype(BF16)
-
-    def send_flow(t, u):
-        u_out[t] = spread(pick_c, flow_rows(u))
-        exchange(u_out.at[t], u_in.at[t], 0, 6, u_ss.at[t], u_rs.at[t])
-
-    def wait_flow(t):
-        whole(u_out.at[t], u_in.at[t], 0, 6, u_ss.at[t], u_rs.at[t]).wait_recv()
-
-
-    def send_weight(t, v):
-        w_out[t] = spread(pick_h, weighted(v))
-        exchange(w_out.at[t], w_in.at[t], 0, w_rows(t), w_ss.at[t], w_rs.at[t])
-
-    def wait_weight(t):
-        whole(w_out.at[t], w_in.at[t], 0, w_rows(t), w_ss.at[t], w_rs.at[t]).wait_recv()
+    class Exchange:
+        def __init__(self, raw, out, inn, zss, zrs, ss, rs, t, rows, shown, spread_one):
+            self.raw, self.out, self.inn, self.t = raw, out, inn, t
+            self.z_sems, self.p_sems = (zss, zrs), (ss.at[t], rs)
+            self.rows, self.shown, self.spread_one = rows, shown, spread_one
+            self.half = rows // 16 * 8
+
+        def z(self, source, region, by, start=0, rows=None, sem=None):
+            rows = self.rows if rows is None else rows
+            sem = region if sem is None else sem
+            return z_copy(self.raw, self.t, source, region, by, start, rows, *self.z_sems, sem)
+
+        def start(self):
+            for by, region in ((2, 3), (-2, 4), (1, 1), (-1, 2)):
+                self.z(0, region, by).start()
+
+        def got(self, region):
+            self.z(region, region, 1).wait_recv()
+
+        def send(self, g):
+            first, tiles = GROUPS[g]
+            for r in range(first, first + tiles):
+                self.spread_one(self.t, r)
+            plane_send(
+                self.out.at[self.t], self.inn.at[self.t], self.p_sems[0],
+                self.p_sems[1].at[self.t, g], first, tiles, 0, self.shown,
+            )
+
+        def forward(self):
+            self.got(3)
+            self.z(3, 7, 2, 0, self.half, 7).start()
+            self.z(3, 5, 1).start()
+            self.got(4)
+            self.z(4, 7, -2, self.half, self.rows - self.half, 8).start()
+            self.z(4, 6, -1).start()
+
+        def near_parts(self):
+            self.got(1)
+            self.got(2)
+            self.send(1)
+
+        def far_parts(self):
+            self.got(5)
+            self.got(6)
+            self.z(7, 7, 1, 0, self.half, 7).wait_recv()
+            self.z(7, 7, 1, self.half, self.rows - self.half, 8).wait_recv()
+            self.send(2)
+
+        def whole(self, g, first, tiles):
+            return plane_whole(
+                self.out.at[self.t], self.inn.at[self.t], self.p_sems[0],
+                self.p_sems[1].at[self.t, g], first, tiles, 0, self.shown,
+            )
+
+        def receive(self):
+            for g in range(3):
+                self.whole(g, *GROUPS[g]).wait_recv()
+            return flat(self.inn[self.t])
+
+        def finish(self):
+            part = (self.t, pl.ds(0, 7), pl.ds(0, self.rows))
+            pltpu.make_async_remote_copy(
+                src_ref=self.raw.at[part],
+                dst_ref=self.raw.at[part],
+                send_sem=self.z_sems[0].at[self.t],
+                recv_sem=self.z_sems[1].at[self.t, 0],
+                device_id=along_z(1),
+                device_id_type=MESH,
+            ).wait_send()
+            self.whole(0, 0, n_z).wait_send()
+
+    def spread_flow(t, r):
+        u_out[t, :, r] = spread(pick_u[r], u_raw[t, r])
+
+    def spread_weight(t, r):
+        w_out[t, :, r] = spread(pick_w[r], w_raw[t, r, 0:96, :])
+
+    plane_target = lax.broadcasted_iota(jnp.int32, (plane, 8, 128), 0) * 2
+
+    def spread_first(t, r):
+        coded = jnp.broadcast_to(w_raw[0, r, 128:129, :], (8, 128)).astype(jnp.int32)
+        lies, level = placed(coded // 2)
+        wanted = jnp.where(
+            matched & (level == zc), 2 * lies + coded % 2 - slot_of, -1000000
+        )
+        hot = jnp.where(wanted[None] == plane_target, 1.0, 0.0).astype(F32)
+        where_to = jnp.broadcast_to(w_raw[0, r, 129:130, :], (8, 128))
+        idw_out[:, r] = jnp.broadcast_to(hot_ids(hot, where_to[None]), (plane, 8, 128))
+        hot = hot.reshape(plane * 8, 128).astype(BF16)
+        pick_w[r, :, 0:128] = hot
+        pick_w[r, :, 128:256] = hot
+        w_out[0, :, r] = spread(pick_w[r], w_raw[0, r, 0:128, :])
+
+    weights = [
+        Exchange(
+            w_raw, w_out, w_in, w_zss, w_zrs, w_ss, w_rs, t,
+            136 if t == 0 else 96, 8 if t == 0 else 6, spread_first if t == 0 else spread_weight,
+        )
+        for t in range(SUBSTEPS)
+    ]
+    flows = [
+        Exchange(u_raw, u_out, u_in, u_zss, u_zrs, u_ss, u_rs, t, 96, 6, spread_flow)
+        for t in range(SUBSTEPS)
+    ]
+
+    def send_ids(g):
+        plane_send(idw_out, idw_in, idw_ss, idw_rs.at[g], *GROUPS[g], 6, 2)
+
+    def picked(id_tiles):
+        first = jnp.broadcast_to(id_tiles[:, 6:7, :], id_tiles.shape)
+        second = jnp.broadcast_to(id_tiles[:, 7:8, :], id_tiles.shape)
+        held = jnp.where((slot_of == 0)[None], first, second)
+        wanted = jnp.where(matched, index + 1, -1).astype(F32)
+        return jnp.where(held == wanted[None], 1.0, 0.0).astype(F32)
+
+    def start_flow(t, u):
+        for a in range(3):
+            u_raw[t, 0, a * 32 : a * 32 + 32, :] = u[a]
+        flows[t].start()
+
+    def start_weight(t, v, pushed):
+        for a in range(3):
+            w_raw[t, 0, a * 32 : a * 32 + 32, :] = rate * ((1.0 - rate) * v[a] + pushed[a])
+        weights[t].start()
+        weights[t].send(0)
 
     def advance(t, v, pushed):
-        wait_flow(t)
-        block = collect(pick_ht, u_in[t], True)
+        block = collect(pick_ht, flows[t].receive(), True)
         updated = []
         for a in range(3):
             u = block[a * 32 : a * 32 + 32]
@@ -396,73 +496,118 @@
     def write_last(i, x, value):
         fluid[i, x] = value
 
-    def fluid_step(t, read, flow, field, write):
-        collide(t, read, flow, field)
-        send_halo(t)
-        stream(t, write)
-
     def field_of(t, before):
-        wait_weight(t)
-        table = collect(pick_ct, w_in[t], True)
+        table = collect(pick_ct, weights[t].receive(), True)
         parts = [table[a * 32 : a * 32 + 32] + solid2 * before[a] for a in range(3)]
         return parts + [solid]
 
-    send_flow(0, flow[1])
+    pl.semaphore_wait(barrier, len(greeted))
+    weights[0].start()
+    plane_send(idh_out, idh_in, idh_ss, idh_rs, 0, n_z, 6, 2)
+    weights[0].send(0)
+    send_ids(0)
+    pick_ht[...] = flat(hot_h).T.astype(BF16)
     pushed = contact_push(velocity)
-    send_weight(1, without_flow(velocity, pushed))
-    pick_ct[...] = hot_c.T.astype(BF16)
-
-    wait_weight(0)
-    table = collect(pick_ct, w_in[0], False)
+
+    weights[0].forward()
+    start_flow(0, flow[1])
+    weights[0].near_parts()
+    send_ids(1)
+
+    idh_whole = plane_whole(idh_out, idh_in, idh_ss, idh_rs, 0, n_z, 6, 2)
+    idh_whole.wait_recv()
+    for r in range(n_z):
+        hot = picked(idh_in[:, r]).reshape(plane * 8, 128).astype(BF16)
+        pick_u[r, :, 0:128] = hot
+        pick_u[r, :, 128:256] = hot
+    flows[0].send(0)
+    weights[0].far_parts()
+    send_ids(2)
+
+    flows[0].forward()
+    start_weight(1, velocity, pushed)
+    flows[0].near_parts()
+
+    for g in range(3):
+        plane_whole(idw_out, idw_in, idw_ss, idw_rs.at[g], *GROUPS[g], 6, 2).wait_recv()
+    hot_c = picked(idw_in[...].reshape(plane * n_z, 8, 128))
+    pick_ct[...] = flat(hot_c).T.astype(BF16)
+    table = weights[0].receive()
+    tail = jnp.where(lax.broadcasted_iota(jnp.int32, table.shape, 0) % 8 < 6, 0.0, table)
+    table = collect(pick_ct, table, False)
     solid = table[96:128]
     field = [table[a * 32 : a * 32 + 32] for a in range(3)] + [solid]
     collide(0, read_first, flow, field)
     send_halo(0)
-    tail = w_in[0].reshape(devices * 8, 128)
-    tail = jnp.where(lax.broadcasted_iota(jnp.int32, (devices * 8, 128), 0) % 8 < 6, 0.0, tail)
+    flows[0].far_parts()
+    weights[1].forward()
     solid2 = collect(pick_ct, tail * tail, False)[96:128]
     stream(0, write_next)
     before = flow[1]
     flow = moments(read_next)
-    send_flow(1, flow[1])
+    start_flow(1, flow[1])
+    flows[1].send(0)
 
     velocity = advance(0, velocity, pushed)
     pushed = contact_push(velocity)
-    send_weight(2, without_flow(velocity, pushed))
-
-    fluid_step(1, read_next, flow, field_of(1, before), write_next)
+    start_weight(2, velocity, pushed)
+    weights[1].near_parts()
+    weights[1].far_parts()
+    flows[1].forward()
+    collide(1, read_next, flow, field_of(1, before))
+    send_halo(1)
+    flows[1].near_parts()
+    weights[2].forward()
+    stream(1, write_next)
     before = flow[1]
     flow = moments(read_next)
-    send_flow(2, flow[1])
+    start_flow(2, flow[1])
+    flows[2].send(0)
+    flows[1].far_parts()
+    weights[2].near_parts()
 
     velocity = advance(1, velocity, pushed)
     pushed = contact_push(velocity)
-    send_weight(3, without_flow(velocity, pushed))
-
-    fluid_step(2, read_next, flow, field_of(2, before), write_next)
+    start_weight(3, velocity, pushed)
+    weights[2].far_parts()
+    flows[2].forward()
+    collide(2, read_next, flow, field_of(2, before))
+    send_halo(2)
+    flows[2].near_parts()
+    weights[3].forward()
+    stream(2, write_next)
     before = flow[1]
     flow = moments(read_next)
-    send_flow(3, flow[1])
+    start_flow(3, flow[1])
+    flows[3].send(0)
+    weights[3].near_parts()
+    flows[2].far_parts()
+    weights[3].far_parts()
+    flows[3].forward()
+    flows[3].near_parts()
 
     velocity = advance(2, velocity, pushed)
     pushed = contact_push(velocity)
-
-    fluid_step(3, read_next, flow, field_of(3, before), write_last)
+    collide(3, read_next, flow, field_of(3, before))
+    send_halo(3)
+    flows[3].far_parts()
+    stream(3, write_last)
 
     velocity = advance(3, velocity, pushed)
     for a in range(3):
         grains[a] = velocity[a]
 
-    id_wait.wait_send()
+    idh_whole.wait_send()
+    plane_whole(idw_out, idw_in, idw_ss, idw_rs.at[0], 0, n_z, 6, 2).wait_send()
     for t in range(SUBSTEPS):
-        whole(u_out.at[t], u_in.at[t], 0, 6, u_ss.at[t], u_rs.at[t]).wait_send()
-        whole(w_out.at[t], w_in.at[t], 0, w_rows(t), w_ss.at[t], w_rs.at[t]).wait_send()
+        weights[t].finish()
+        flows[t].finish()
         halo_whole(t).wait_send()
 
 
 def solution(mesh):
     n_gx, n_gy = mesh.shape["gx"], mesh.shape["gy"]
-    devices = n_gx * n_gy
+    plane = n_gx // 8 * n_gy
     vmem = pl.BlockSpec(memory_space=pltpu.VMEM)
     smem = pl.BlockSpec(memory_space=pltpu.SMEM)
     dma = pltpu.SemaphoreType.DMA
@@ -479,27 +624,27 @@
             scratch_shapes=[
                 pltpu.VMEM((608, 128), F32),
                 pltpu.VMEM((608, 128), F32),
-                pltpu.VMEM((devices * 8, 256), BF16),
-                pltpu.VMEM((128, devices * 8), BF16),
-                pltpu.VMEM((devices * 8, 256), BF16),
-                pltpu.VMEM((128, devices * 8), BF16),
-                pltpu.VMEM((devices, 8, 128), F32),
-                pltpu.VMEM((devices, 8, 128), F32),
-                pltpu.VMEM((SUBSTEPS, devices, 8, 128), F32),
-                pltpu.VMEM((SUBSTEPS, devices, 8, 128), F32),
-                pltpu.VMEM((SUBSTEPS, devices, 8, 128), F32),
-                pltpu.VMEM((SUBSTEPS, devices, 8, 128), F32),
+                pltpu.VMEM((8, plane * 8, 256), BF16),
+                pltpu.VMEM((8, plane * 8, 256), BF16),
+                pltpu.VMEM((128, plane * 64), BF16),
+                pltpu.VMEM((128, plane * 64), BF16),
+            ]
+            + [pltpu.VMEM((plane, 8, 8, 128), F32)] * 4
+            + [
+                pltpu.VMEM((SUBSTEPS, 8, 96, 128), F32),
+                pltpu.VMEM((SUBSTEPS, 8, 136, 128), F32),
+            ]
+            + [pltpu.VMEM((SUBSTEPS, plane, 8, 8, 128), F32)] * 4
+            + [
                 pltpu.VMEM((SUBSTEPS, 17, 8, 128), F32),
                 pltpu.VMEM((SUBSTEPS, 25, 8, 128), F32),
                 dma,
                 dma,
-                dma((SUBSTEPS,)),
-                dma((SUBSTEPS,)),
-                dma((SUBSTEPS,)),
-                dma((SUBSTEPS,)),
-                dma((SUBSTEPS,)),
-                dma((SUBSTEPS,)),
-            ],
+                dma,
+                dma((3,)),
+            ]
+            + [dma((SUBSTEPS,)), dma((SUBSTEPS, 9)), dma((SUBSTEPS,)), dma((SUBSTEPS, 3))] * 2
+            + [dma((SUBSTEPS,)), dma((SUBSTEPS,))],
             compiler_params=pltpu.CompilerParams(
                 collective_id=0, has_side_effects=True, vmem_limit_bytes=48 << 20
             ),

time: 112 us -> 94.9 us (0.85)
  Pallas kernels: 105 us -> 88 us
    pallas_call x1, Pallas kernels: 105 us -> 88 us  [body(): pl.pallas_call(lambda *refs: kernel(n_gx, n_gy, *refs), out_shape=(jax.Sh...]
where the time goes in v2:
time: 94.9 us; the launch traced here: 94.5 us
  Pallas kernels  88 us (93%)
  local copies, waits for them, and re-layouts  5.9 us (6%)
    pallas_call x1, Pallas kernels, body(): pl.pallas_call(lambda *refs: kernel(n_gx, n_gy, *refs), out_shape=(jax.Sh...  88 us
    unnamed x14, local copies, waits for them, and re-layouts  5.9 us

profile of v2, /device:TPU:1, one launch (start us, length us, event | category | flops | bytes accessed | tf_op | source)
XLA Modules:
  0.0 94.5 jit_solution(5654199193148859501)
XLA Ops:
  0.6 0.0 copy-start
  0.6 1.0 %copy-done = f32[19,4,8,128]{3,2,1,0:T(8,128)S(1)} copy-done((f32[19,4,8,128]{3,2,1,0:T(8,128)S(1)}, f32[19,4,8,128]{3,2,1,0:T(8,128)}, u32[]{:S(2)}) %copy-start) | copy-done | bytes 311320
  1.6 0.0 copy-start.1
  1.6 0.8 copy-done.1
  2.4 0.0 copy-start.2
  2.4 0.7 copy-done.2
  3.1 0.0 copy-start.3
  3.1 0.7 copy-done.3
  3.8 0.0 copy-start.4
  3.8 0.7 copy-done.4
  4.6 0.0 copy-start.5
  4.6 0.7 copy-done.5
  5.2 88.0 %bed.1 = (f32[19,4,8,128]{3,2,1,0:T(8,128)S(1)}, f32[3,32,128]{2,1,0:T(8,128)S(1)}) custom-call(f32[19,4,8,128]{3,2,1,0:T(8,128)S(1)} %copy-done, f32[3,32,128]{2,1,0:T(8,128)S(1)} %copy-done.1, f32[32,128]{1,0:T(8,128)S(1)} %copy-done.2, s32[32,128]{1,0:T(8,128)S(1)} %copy-done.3, s32[32,32]{1,0:T(8,128)S(1)} %copy-done.4, s32[32]{0:T(128)S(1)} %copy-done.5), custom_call_target="tpu_custom_call" | custom-call | tf_op jit(solution)/shard_map/bed/pallas_call | solution.py:616
  93.2 0.7 copy.10
  93.9 0.6 copy.11
Async XLA Ops:
  0.6 1.0 %copy-start = (f32[19,4,8,128]{3,2,1,0:T(8,128)S(1)}, f32[19,4,8,128]{3,2,1,0:T(8,128)}, u32[]{:S(2)}) copy-start(f32[19,4,8,128]{3,2,1,0:T(8,128)} %refs_0_.1) | copy-start | bytes 933892
  1.6 0.8 copy-start.1
  2.4 0.7 copy-start.2
  3.1 0.7 copy-start.3
  3.8 0.7 copy-start.4
  4.6 0.7 copy-start.5

commit v3 on v2

--- a/solution.py
+++ b/solution.py
@@ -29,6 +29,17 @@
 Z_DOWN = [6, 13, 12, 17, 16]
 SOURCE = [0, -1, 1, -2, 2, -3, 3, 4]
 GROUPS = [(0, 1), (1, 4), (5, 3)]
+
+ORDER = [
+    "start_w0", "own_w0", "pick_h", "on_w0", "pick_u", "start_u0", "start_w1",
+    "near_w0", "far_w0", "own_u0", "own_w1", "on_u0", "near_u0", "on_w1",
+    "far_u0", "near_w1", "pick_c", "collide0", "far_w1", "grain0", "squares",
+    "stream0", "collide1", "own_w2", "on_w2", "own_u1", "near_w2", "on_u1",
+    "near_u1", "stream1", "far_w2", "far_u1", "own_u2", "on_u2", "collide2",
+    "grain1", "near_u2", "own_w3", "on_w3", "stream2", "near_w3", "far_w3",
+    "far_u2", "on_u3", "near_u3", "own_u3", "far_u3", "collide3", "grain2",
+    "grain3", "stream3",
+]
 
 F32 = jnp.float32
 BF16 = jnp.bfloat16
@@ -349,7 +360,6 @@
         for a in range(3):
             w_raw[t, 0, a * 32 : a * 32 + 32, :] = rate * ((1.0 - rate) * v[a] + pushed[a])
         weights[t].start()
-        weights[t].send(0)
 
     def advance(t, v, pushed):
         block = collect(pick_ht, flows[t].receive(), True)
@@ -496,106 +506,92 @@
     def write_last(i, x, value):
         fluid[i, x] = value
 
-    def field_of(t, before):
-        table = collect(pick_ct, weights[t].receive(), True)
-        parts = [table[a * 32 : a * 32 + 32] + solid2 * before[a] for a in range(3)]
-        return parts + [solid]
+    idh_whole = plane_whole(idh_out, idh_in, idh_ss, idh_rs, 0, n_z, 6, 2)
+    flow_at = [flow] + [None] * SUBSTEPS
+    field_at = [None] * SUBSTEPS
+    velocity_at = [velocity] + [None] * SUBSTEPS
+    push_at = [contact_push(velocity)] + [None] * SUBSTEPS
+    solid_at = {}
+
+    def start_weights():
+        weights[0].start()
+        plane_send(idh_out, idh_in, idh_ss, idh_rs, 0, n_z, 6, 2)
+
+    def pick_for_flows():
+        idh_whole.wait_recv()
+        for r in range(n_z):
+            hot = picked(idh_in[:, r]).reshape(plane * 8, 128).astype(BF16)
+            pick_u[r, :, 0:128] = hot
+            pick_u[r, :, 128:256] = hot
+
+    def pick_for_bins():
+        pick_ht[...] = flat(hot_h).T.astype(BF16)
+
+    def pick_for_columns():
+        for g in range(3):
+            plane_whole(idw_out, idw_in, idw_ss, idw_rs.at[g], *GROUPS[g], 6, 2).wait_recv()
+        hot_c = picked(idw_in[...].reshape(plane * n_z, 8, 128))
+        pick_ct[...] = flat(hot_c).T.astype(BF16)
+
+    def squares():
+        tail = flat(w_in[0])
+        tail = jnp.where(lax.broadcasted_iota(jnp.int32, tail.shape, 0) % 8 < 6, 0.0, tail)
+        solid_at[2] = collect(pick_ct, tail * tail, False)[96:128]
+
+    def fluid_first(t):
+        rows = weights[t].receive()
+        table = collect(pick_ct, rows, t > 0)
+        if t == 0:
+            solid_at[1] = table[96:128]
+        parts = [table[a * 32 : a * 32 + 32] for a in range(3)]
+        if t > 0:
+            before = flow_at[t - 1][1]
+            parts = [parts[a] + solid_at[2] * before[a] for a in range(3)]
+        collide(t, read_first if t == 0 else read_next, flow_at[t], parts + [solid_at[1]])
+        send_halo(t)
+
+    def fluid_last(t):
+        if t == SUBSTEPS - 1:
+            stream(t, write_last)
+            return
+        stream(t, write_next)
+        flow_at[t + 1] = moments(read_next)
+        start_flow(t + 1, flow_at[t + 1][1])
+
+    def grain(t):
+        velocity_at[t + 1] = advance(t, velocity_at[t], push_at[t])
+        if t < SUBSTEPS - 1:
+            push_at[t + 1] = contact_push(velocity_at[t + 1])
+        else:
+            for a in range(3):
+                grains[a] = velocity_at[t + 1][a]
+        if t + 2 < SUBSTEPS:
+            start_weight(t + 2, velocity_at[t + 1], push_at[t + 1])
+
+    steps = {
+        "start_w0": start_weights,
+        "start_u0": lambda: start_flow(0, flow_at[0][1]),
+        "start_w1": lambda: start_weight(1, velocity_at[0], push_at[0]),
+        "pick_u": pick_for_flows,
+        "pick_h": pick_for_bins,
+        "pick_c": pick_for_columns,
+        "squares": squares,
+    }
+    for t in range(SUBSTEPS):
+        steps[f"collide{t}"] = lambda t=t: fluid_first(t)
+        steps[f"stream{t}"] = lambda t=t: fluid_last(t)
+        steps[f"grain{t}"] = lambda t=t: grain(t)
+        for name, one in (("w", weights[t]), ("u", flows[t])):
+            ids = send_ids if name == "w" and t == 0 else lambda g: None
+            steps[f"own_{name}{t}"] = lambda one=one, ids=ids: (one.send(0), ids(0))
+            steps[f"on_{name}{t}"] = lambda one=one: one.forward()
+            steps[f"near_{name}{t}"] = lambda one=one, ids=ids: (one.near_parts(), ids(1))
+            steps[f"far_{name}{t}"] = lambda one=one, ids=ids: (one.far_parts(), ids(2))
 
     pl.semaphore_wait(barrier, len(greeted))
-    weights[0].start()
-    plane_send(idh_out, idh_in, idh_ss, idh_rs, 0, n_z, 6, 2)
-    weights[0].send(0)
-    send_ids(0)
-    pick_ht[...] = flat(hot_h).T.astype(BF16)
-    pushed = contact_push(velocity)
-
-    weights[0].forward()
-    start_flow(0, flow[1])
-    weights[0].near_parts()
-    send_ids(1)
-
-    idh_whole = plane_whole(idh_out, idh_in, idh_ss, idh_rs, 0, n_z, 6, 2)
-    idh_whole.wait_recv()
-    for r in range(n_z):
-        hot = picked(idh_in[:, r]).reshape(plane * 8, 128).astype(BF16)
-        pick_u[r, :, 0:128] = hot
-        pick_u[r, :, 128:256] = hot
-    flows[0].send(0)
-    weights[0].far_parts()
-    send_ids(2)
-
-    flows[0].forward()
-    start_weight(1, velocity, pushed)
-    flows[0].near_parts()
-
-    for g in range(3):
-        plane_whole(idw_out, idw_in, idw_ss, idw_rs.at[g], *GROUPS[g], 6, 2).wait_recv()
-    hot_c = picked(idw_in[...].reshape(plane * n_z, 8, 128))
-    pick_ct[...] = flat(hot_c).T.astype(BF16)
-    table = weights[0].receive()
-    tail = jnp.where(lax.broadcasted_iota(jnp.int32, table.shape, 0) % 8 < 6, 0.0, table)
-    table = collect(pick_ct, table, False)
-    solid = table[96:128]
-    field = [table[a * 32 : a * 32 + 32] for a in range(3)] + [solid]
-    collide(0, read_first, flow, field)
-    send_halo(0)
-    flows[0].far_parts()
-    weights[1].forward()
-    solid2 = collect(pick_ct, tail * tail, False)[96:128]
-    stream(0, write_next)
-    before = flow[1]
-    flow = moments(read_next)
-    start_flow(1, flow[1])
-    flows[1].send(0)
-
-    velocity = advance(0, velocity, pushed)
-    pushed = contact_push(velocity)
-    start_weight(2, velocity, pushed)
-    weights[1].near_parts()
-    weights[1].far_parts()
-    flows[1].forward()
-    collide(1, read_next, flow, field_of(1, before))
-    send_halo(1)
-    flows[1].near_parts()
-    weights[2].forward()
-    stream(1, write_next)
-    before = flow[1]
-    flow = moments(read_next)
-    start_flow(2, flow[1])
-    flows[2].send(0)
-    flows[1].far_parts()
-    weights[2].near_parts()
-
-    velocity = advance(1, velocity, pushed)
-    pushed = contact_push(velocity)
-    start_weight(3, velocity, pushed)
-    weights[2].far_parts()
-    flows[2].forward()
-    collide(2, read_next, flow, field_of(2, before))
-    send_halo(2)
-    flows[2].near_parts()
-    weights[3].forward()
-    stream(2, write_next)
-    before = flow[1]
-    flow = moments(read_next)
-    start_flow(3, flow[1])
-    flows[3].send(0)
-    weights[3].near_parts()
-    flows[2].far_parts()
-    weights[3].far_parts()
-    flows[3].forward()
-    flows[3].near_parts()
-
-    velocity = advance(2, velocity, pushed)
-    pushed = contact_push(velocity)
-    collide(3, read_next, flow, field_of(3, before))
-    send_halo(3)
-    flows[3].far_parts()
-    stream(3, write_last)
-
-    velocity = advance(3, velocity, pushed)
-    for a in range(3):
-        grains[a] = velocity[a]
+    assert sorted(ORDER) == sorted(steps)
+    for name in ORDER:
+        steps[name]()
 
     idh_whole.wait_send()
     plane_whole(idw_out, idw_in, idw_ss, idw_rs.at[0], 0, n_z, 6, 2).wait_send()

time: 94.9 us -> 86.3 us (0.909)
  Pallas kernels: 88 us -> 79.3 us
    pallas_call x1, Pallas kernels: 88 us -> 79.3 us  [body(): pl.pallas_call(lambda *refs: kernel(n_gx, n_gy, *refs), out_shape=(jax.Sh...]
where the time goes in v3:
time: 86.3 us; the launch traced here: 85.9 us
  Pallas kernels  79.3 us (92%)
  local copies, waits for them, and re-layouts  5.9 us (7%)
    pallas_call x1, Pallas kernels, body(): pl.pallas_call(lambda *refs: kernel(n_gx, n_gy, *refs), out_shape=(jax.Sh...  79.3 us
    unnamed x14, local copies, waits for them, and re-layouts  5.9 us

profile of v3, /device:TPU:1, one launch (start us, length us, event | category | flops | bytes accessed | tf_op | source)
XLA Modules:
  0.0 85.9 jit_solution(4447492092112847154)
XLA Ops:
  0.6 0.0 copy-start
  0.6 1.0 %copy-done = f32[19,4,8,128]{3,2,1,0:T(8,128)S(1)} copy-done((f32[19,4,8,128]{3,2,1,0:T(8,128)S(1)}, f32[19,4,8,128]{3,2,1,0:T(8,128)}, u32[]{:S(2)}) %copy-start) | copy-done | bytes 311320
  1.6 0.0 copy-start.1
  1.6 0.8 copy-done.1
  2.4 0.0 copy-start.2
  2.4 0.7 copy-done.2
  3.1 0.0 copy-start.3
  3.1 0.7 copy-done.3
  3.8 0.0 copy-start.4
  3.8 0.7 copy-done.4
  4.6 0.0 copy-start.5
  4.6 0.7 copy-done.5
  5.2 79.3 %bed.1 = (f32[19,4,8,128]{3,2,1,0:T(8,128)S(1)}, f32[3,32,128]{2,1,0:T(8,128)S(1)}) custom-call(f32[19,4,8,128]{3,2,1,0:T(8,128)S(1)} %copy-done, f32[3,32,128]{2,1,0:T(8,128)S(1)} %copy-done.1, f32[32,128]{1,0:T(8,128)S(1)} %copy-done.2, s32[32,128]{1,0:T(8,128)S(1)} %copy-done.3, s32[32,32]{1,0:T(8,128)S(1)} %copy-done.4, s32[32]{0:T(128)S(1)} %copy-done.5), custom_call_target="tpu_custom_call" | custom-call | tf_op jit(solution)/shard_map/bed/pallas_call | solution.py:612
  84.6 0.7 copy.10
  85.3 0.6 copy.11
Async XLA Ops:
  0.6 1.0 %copy-start = (f32[19,4,8,128]{3,2,1,0:T(8,128)S(1)}, f32[19,4,8,128]{3,2,1,0:T(8,128)}, u32[]{:S(2)}) copy-start(f32[19,4,8,128]{3,2,1,0:T(8,128)} %refs_0_.1) | copy-start | bytes 933892
  1.6 0.8 copy-start.1
  2.4 0.7 copy-start.2
  3.1 0.7 copy-start.3
  3.8 0.7 copy-start.4
  4.6 0.7 copy-start.5

commit v4 on v3

--- a/solution.py
+++ b/solution.py
@@ -29,16 +29,17 @@
 Z_DOWN = [6, 13, 12, 17, 16]
 SOURCE = [0, -1, 1, -2, 2, -3, 3, 4]
 GROUPS = [(0, 1), (1, 4), (5, 3)]
+RELAYS = [
+    (0, 0, 0, 0, 1), (1, 0, 1, 0, 1), (2, 0, 2, 0, 1), (3, 0, 3, 0, 1), (4, 0, 4, 0, 1),
+    (3, 1, 5, 0, 1), (4, -1, 6, 0, 1), (3, 2, 7, 0, 2), (4, -2, 7, 1, 2),
+]
 
 ORDER = [
-    "start_w0", "own_w0", "pick_h", "on_w0", "pick_u", "start_u0", "start_w1",
-    "near_w0", "far_w0", "own_u0", "own_w1", "on_u0", "near_u0", "on_w1",
-    "far_u0", "near_w1", "pick_c", "collide0", "far_w1", "grain0", "squares",
-    "stream0", "collide1", "own_w2", "on_w2", "own_u1", "near_w2", "on_u1",
-    "near_u1", "stream1", "far_w2", "far_u1", "own_u2", "on_u2", "collide2",
-    "grain1", "near_u2", "own_w3", "on_w3", "stream2", "near_w3", "far_w3",
-    "far_u2", "on_u3", "near_u3", "own_u3", "far_u3", "collide3", "grain2",
-    "grain3", "stream3",
+    "start_w0", "own_w0", "relay_w0", "start_u0", "pick_u", "start_w1", "own_u0",
+    "relay_u0", "own_w1", "pick_h", "relay_w1", "pick_c", "collide0", "grain0",
+    "own_w2", "stream0", "own_u1", "squares", "relay_w2", "collide1", "relay_u1",
+    "stream1", "own_u2", "collide2", "grain1", "own_w3", "relay_u2", "stream2",
+    "relay_w3", "own_u3", "relay_u3", "collide3", "grain2", "grain3", "stream3",
 ]
 
 F32 = jnp.float32
@@ -81,14 +82,18 @@
     south, north = (gy + n_gy - 1) % n_gy, (gy + 1) % n_gy
     beyond = 1 - gz
     across = [(gx, gy), (east, gy), (west, gy), (gx, north), (gx, south)]
-    corners = [(east, north), (west, south), (east, south), (west, north)]
 
     barrier = pltpu.get_barrier_semaphore()
-    greeted = [along_z(by) for by in (2, -2, 1, -1)]
-    for m in range(plane - 1, 0, -1):
+    def beside(m, by):
         px, py = in_plane(m)
-        greeted.append((px * n_z + zc, py, gz))
-    greeted += [(px, py, gz) for px, py in [(east, gy), (west, gy)] + corners]
+        return (px * n_z + (zc + by + n_z) % n_z, py, gz)
+
+    greeted = [
+        beside(m, by)
+        for by in (2, -2, 1, -1, 0)
+        for m in range(plane - 1, -1, -1)
+        if m or by
+    ]
     greeted += [(px, py, beyond) for px, py in across]
     for device in greeted:
         pl.semaphore_signal(barrier, inc=1, device_id=device, device_id_type=MESH)
@@ -105,25 +110,42 @@
         )
 
     def plane_send(out, inn, ss, rs, first, tiles, row, rows):
-        part = (pl.ds(first, tiles), pl.ds(row, rows))
-
-        def send(i, carry):
-            px, py = in_plane(plane - 1 - i)
+        some, part = pl.ds(first, tiles), pl.ds(row, rows)
+        for m in range(plane - 1, 0, -1):
+            px, py = in_plane(m)
             pltpu.make_async_remote_copy(
-                src_ref=out.at[(px * n_gy + py,) + part],
-                dst_ref=inn.at[(me,) + part],
+                src_ref=out.at[some, px * n_gy + py, part],
+                dst_ref=inn.at[some, me, part],
                 send_sem=ss,
                 recv_sem=rs,
                 device_id=(px * n_z + zc, py, gz),
                 device_id_type=MESH,
             ).start()
-            return carry
-
-        lax.fori_loop(0, plane - 1, send, 0)
-        inn[me, pl.ds(first, tiles)] = out[me, pl.ds(first, tiles)]
+        inn[some, me] = out[some, me]
+
+    def side_send(out, inn, ss, rs, k, row, rows):
+        _, by, region, first, step = RELAYS[k]
+        part = pl.ds(row, rows)
+        for m in range(plane - 1, -1, -1):
+            if step == 2:
+                if m % 2:
+                    continue
+                px, py = in_plane(m)
+                py = py // 2 * 2 + first
+            else:
+                px, py = in_plane(m)
+            pltpu.make_async_remote_copy(
+                src_ref=out.at[k, (px * n_gy + py) // step, part],
+                dst_ref=inn.at[region, me, part],
+                send_sem=ss,
+                recv_sem=rs,
+                device_id=(px * n_z + (zc + by + n_z) % n_z, py, gz),
+                device_id_type=MESH,
+            ).start()
 
     def plane_whole(out, inn, ss, rs, first, tiles, row, rows):
-        span = (pl.ds(0, plane - 1), pl.ds(first, tiles), pl.ds(row, rows))
+        devices = plane - 1 if first < 5 else plane
+        span = (pl.ds(first, tiles), pl.ds(0, devices), pl.ds(row, rows))
         return pltpu.make_async_remote_copy(
             src_ref=out.at[span],
             dst_ref=inn.at[span],
@@ -166,13 +188,13 @@
     region_of = jnp.zeros((8, 128), jnp.int32)
     for r, by in enumerate(SOURCE):
         region_of = jnp.where(away == by % n_z, r, region_of)
-    code = jnp.where(matched, 2 * (side * n_z + region_of) + rank - slot_of, -1000000)
+    code = jnp.where(matched, 2 * (region_of * plane + side) + rank - slot_of, -1000000)
     target = lax.broadcasted_iota(jnp.int32, (plane * n_z, 8, 128), 0) * 2
     hot_h = jnp.where(code[None] == target, 1.0, 0.0).astype(F32)
     column = (local + 1).astype(F32)
     idh_out[...] = jnp.broadcast_to(
         hot_ids(hot_h, column[None]), (plane * n_z, 8, 128)
-    ).reshape(plane, n_z, 8, 128)
+    ).reshape(n_z, plane, 8, 128)
 
     def spread(pick, table):
         if table.shape[0] == 96:
@@ -180,17 +202,19 @@
         high, low = split(table)
         both = jnp.concatenate([high, low], axis=0)
         rows = jnp.dot(pick, both, preferred_element_type=F32)
-        return rows.reshape(plane, 8, 128)
-
-    def collect(pick_t, rows, masked):
+        return rows.reshape(-1, 8, 128)
+
+    def collect(table, rows, masked):
         if masked:
             inside = lax.broadcasted_iota(jnp.int32, rows.shape, 0) % 8 < 6
             rows = jnp.where(inside, rows, 0.0)
-        high, low = split(rows)
-        table = pick_t[...]
-        return jnp.dot(table, high, preferred_element_type=F32) + jnp.dot(
-            table, low, preferred_element_type=F32
-        )
+        both = jnp.concatenate(split(rows), axis=1)
+        sums = jnp.dot(table, both, preferred_element_type=F32)
+        return sums[:, 0:128] + sums[:, 128:256]
+
+    def columns_of(g):
+        first, tiles = GROUPS[g]
+        return slice(first * plane * 8, (first + tiles) * plane * 8)
 
     def flat(tiles):
         return tiles.reshape(plane * n_z * 8, 128)
@@ -239,64 +263,63 @@
     class Exchange:
         def __init__(self, raw, out, inn, zss, zrs, ss, rs, t, rows, shown, spread_one):
             self.raw, self.out, self.inn, self.t = raw, out, inn, t
-            self.z_sems, self.p_sems = (zss, zrs), (ss.at[t], rs)
+            self.z_sems, self.p_sems = (zss, zrs), (ss, rs)
             self.rows, self.shown, self.spread_one = rows, shown, spread_one
-            self.half = rows // 16 * 8
-
-        def z(self, source, region, by, start=0, rows=None, sem=None):
-            rows = self.rows if rows is None else rows
-            sem = region if sem is None else sem
-            return z_copy(self.raw, self.t, source, region, by, start, rows, *self.z_sems, sem)
+
+        def z(self, region, by):
+            return z_copy(self.raw, self.t, 0, region, by, 0, self.rows, *self.z_sems, region)
 
         def start(self):
             for by, region in ((2, 3), (-2, 4), (1, 1), (-1, 2)):
-                self.z(0, region, by).start()
+                self.z(region, by).start()
 
         def got(self, region):
-            self.z(region, region, 1).wait_recv()
+            self.z(region, 1).wait_recv()
 
         def send(self, g):
             first, tiles = GROUPS[g]
-            for r in range(first, first + tiles):
-                self.spread_one(self.t, r)
+            for k in range(first, first + tiles):
+                self.spread_one(self.t, k)
             plane_send(
-                self.out.at[self.t], self.inn.at[self.t], self.p_sems[0],
+                self.out.at[self.t], self.inn.at[self.t], self.p_sems[0].at[self.t, 0],
                 self.p_sems[1].at[self.t, g], first, tiles, 0, self.shown,
             )
 
-        def forward(self):
+        def send_far(self, k):
+            self.spread_one(self.t, k)
+            side_send(
+                self.out.at[self.t], self.inn.at[self.t], self.p_sems[0].at[self.t, 1],
+                self.p_sems[1].at[self.t, 2], k, 0, self.shown,
+            )
+
+        def relay(self):
             self.got(3)
-            self.z(3, 7, 2, 0, self.half, 7).start()
-            self.z(3, 5, 1).start()
+            self.send_far(7)
+            self.send_far(5)
             self.got(4)
-            self.z(4, 7, -2, self.half, self.rows - self.half, 8).start()
-            self.z(4, 6, -1).start()
-
-        def near_parts(self):
+            self.send_far(8)
+            self.send_far(6)
             self.got(1)
             self.got(2)
             self.send(1)
 
-        def far_parts(self):
-            self.got(5)
-            self.got(6)
-            self.z(7, 7, 1, 0, self.half, 7).wait_recv()
-            self.z(7, 7, 1, self.half, self.rows - self.half, 8).wait_recv()
-            self.send(2)
-
         def whole(self, g, first, tiles):
             return plane_whole(
-                self.out.at[self.t], self.inn.at[self.t], self.p_sems[0],
+                self.out.at[self.t], self.inn.at[self.t], self.p_sems[0].at[self.t, g // 2],
                 self.p_sems[1].at[self.t, g], first, tiles, 0, self.shown,
             )
 
-        def receive(self):
-            for g in range(3):
-                self.whole(g, *GROUPS[g]).wait_recv()
-            return flat(self.inn[self.t])
+        def collected(self, pick_t, masked):
+            total = None
+            for g, (first, tiles) in enumerate(GROUPS):
+                self.whole(g, first, tiles).wait_recv()
+                rows = self.inn[self.t, pl.ds(first, tiles)].reshape(tiles * plane * 8, 128)
+                part = collect(pick_t[:, columns_of(g)], rows, masked)
+                total = part if total is None else total + part
+            return total
 
         def finish(self):
-            part = (self.t, pl.ds(0, 7), pl.ds(0, self.rows))
+            part = (self.t, pl.ds(0, 4), pl.ds(0, self.rows))
             pltpu.make_async_remote_copy(
                 src_ref=self.raw.at[part],
                 dst_ref=self.raw.at[part],
@@ -305,29 +328,44 @@
                 device_id=along_z(1),
                 device_id_type=MESH,
             ).wait_send()
-            self.whole(0, 0, n_z).wait_send()
-
-    def spread_flow(t, r):
-        u_out[t, :, r] = spread(pick_u[r], u_raw[t, r])
-
-    def spread_weight(t, r):
-        w_out[t, :, r] = spread(pick_w[r], w_raw[t, r, 0:96, :])
-
-    plane_target = lax.broadcasted_iota(jnp.int32, (plane, 8, 128), 0) * 2
-
-    def spread_first(t, r):
-        coded = jnp.broadcast_to(w_raw[0, r, 128:129, :], (8, 128)).astype(jnp.int32)
+            self.whole(0, 0, 5).wait_send()
+            self.whole(2, 5, 3).wait_send()
+
+    def put(ref, index, k, value):
+        if RELAYS[k][4] == 1:
+            ref[index + (k,)] = value
+        else:
+            ref[index + (k, slice(0, plane // 2))] = value
+
+    def pick_of(pick, k):
+        return pick[k] if RELAYS[k][4] == 1 else pick[k, 0 : plane * 4]
+
+    def keep_pick(pick, k, hot):
+        rows = hot.shape[0] * 8
+        hot = hot.reshape(rows, 128).astype(BF16)
+        pick[k, 0:rows, 0:128] = hot
+        pick[k, 0:rows, 128:256] = hot
+
+    def spread_flow(t, k):
+        put(u_out, (t,), k, spread(pick_of(pick_u, k), u_raw[t, RELAYS[k][0]]))
+
+    def spread_weight(t, k):
+        put(w_out, (t,), k, spread(pick_of(pick_w, k), w_raw[t, RELAYS[k][0], 0:96, :]))
+
+    def spread_first(t, k):
+        raw, by, _, first, step = RELAYS[k]
+        coded = jnp.broadcast_to(w_raw[0, raw, 128:129, :], (8, 128)).astype(jnp.int32)
         lies, level = placed(coded // 2)
         wanted = jnp.where(
-            matched & (level == zc), 2 * lies + coded % 2 - slot_of, -1000000
+            matched & (level == (zc + by + n_z) % n_z), 2 * lies + coded % 2 - slot_of, -1000000
         )
-        hot = jnp.where(wanted[None] == plane_target, 1.0, 0.0).astype(F32)
-        where_to = jnp.broadcast_to(w_raw[0, r, 129:130, :], (8, 128))
-        idw_out[:, r] = jnp.broadcast_to(hot_ids(hot, where_to[None]), (plane, 8, 128))
-        hot = hot.reshape(plane * 8, 128).astype(BF16)
-        pick_w[r, :, 0:128] = hot
-        pick_w[r, :, 128:256] = hot
-        w_out[0, :, r] = spread(pick_w[r], w_raw[0, r, 0:128, :])
+        shape = (plane // step, 8, 128)
+        target = 2 * (lax.broadcasted_iota(jnp.int32, shape, 0) * step + first)
+        hot = jnp.where(wanted[None] == target, 1.0, 0.0).astype(F32)
+        where_to = jnp.broadcast_to(w_raw[0, raw, 129:130, :], (8, 128))
+        put(idw_out, (), k, jnp.broadcast_to(hot_ids(hot, where_to[None]), shape))
+        keep_pick(pick_w, k, hot)
+        put(w_out, (0,), k, spread(pick_of(pick_w, k), w_raw[0, raw, 0:128, :]))
 
     weights = [
         Exchange(
@@ -342,7 +380,11 @@
     ]
 
     def send_ids(g):
-        plane_send(idw_out, idw_in, idw_ss, idw_rs.at[g], *GROUPS[g], 6, 2)
+        plane_send(idw_out, idw_in, idw_ss.at[0], idw_rs.at[g], *GROUPS[g], 6, 2)
+
+    def send_ids_far():
+        for k in range(5, 9):
+            side_send(idw_out, idw_in, idw_ss.at[1], idw_rs.at[2], k, 6, 2)
 
     def picked(id_tiles):
         first = jnp.broadcast_to(id_tiles[:, 6:7, :], id_tiles.shape)
@@ -362,7 +404,7 @@
         weights[t].start()
 
     def advance(t, v, pushed):
-        block = collect(pick_ht, flows[t].receive(), True)
+        block = flows[t].collected(pick_ht, True)
         updated = []
         for a in range(3):
             u = block[a * 32 : a * 32 + 32]
@@ -405,11 +447,20 @@
         for n in range(5):
             halo_out[t, n] = tile(X_UP[n], 3)
             halo_out[t, 5 + n] = tile(X_DOWN[n], 0)
+        halo_copy(t, 1, 1, 16, east, north, gz).start()
+        halo_copy(t, 6, 1, 17, west, south, gz).start()
+        halo_copy(t, 2, 1, 18, east, south, gz).start()
+        halo_copy(t, 7, 1, 19, west, north, gz).start()
+        halo_copy(t, 0, 5, 0, east, gy, gz).start()
+        halo_copy(t, 5, 5, 5, west, gy, gz).start()
+        for n in range(5):
             half = pl.ds((n % 2) * 4, 4)
             halo_out[t, 10 + n // 2, half, :] = post[pl.ds(Y_UP[n] * 32 + 7, 4, stride=8), :]
             halo_out[t, 13 + n // 2, half, :] = post[pl.ds(Y_DOWN[n] * 32, 4, stride=8), :]
         halo_out[t, 12, 4:8, :] = jnp.zeros((4, 128), F32)
         halo_out[t, 15, 4:8, :] = jnp.zeros((4, 128), F32)
+        halo_copy(t, 10, 3, 10, gx, north, gz).start()
+        halo_copy(t, 13, 3, 13, gx, south, gz).start()
         packed = jnp.zeros((8, 128), F32)
         for n in range(5):
             for x in range(4):
@@ -418,14 +469,6 @@
                 down = pltpu.roll(tile(Z_DOWN[n], x), k, 1) if k else tile(Z_DOWN[n], x)
                 packed = jnp.where(lane == k, jnp.where(gz == 0, up, down), packed)
         halo_out[t, 16] = packed
-        halo_copy(t, 0, 5, 0, east, gy, gz).start()
-        halo_copy(t, 5, 5, 5, west, gy, gz).start()
-        halo_copy(t, 10, 3, 10, gx, north, gz).start()
-        halo_copy(t, 13, 3, 13, gx, south, gz).start()
-        halo_copy(t, 1, 1, 16, east, north, gz).start()
-        halo_copy(t, 6, 1, 17, west, south, gz).start()
-        halo_copy(t, 2, 1, 18, east, south, gz).start()
-        halo_copy(t, 7, 1, 19, west, north, gz).start()
         for n, (px, py) in enumerate(across):
             halo_copy(t, 16, 1, 20 + n, px, py, beyond).start()
 
@@ -506,7 +549,10 @@
     def write_last(i, x, value):
         fluid[i, x] = value
 
-    idh_whole = plane_whole(idh_out, idh_in, idh_ss, idh_rs, 0, n_z, 6, 2)
+    idh_whole = [
+        plane_whole(idh_out, idh_in, idh_ss.at[n], idh_rs.at[n], first, tiles, 6, 2)
+        for n, (first, tiles) in enumerate([(0, 5), (5, 3)])
+    ]
     flow_at = [flow] + [None] * SUBSTEPS
     field_at = [None] * SUBSTEPS
     velocity_at = [velocity] + [None] * SUBSTEPS
@@ -515,32 +561,45 @@
 
     def start_weights():
         weights[0].start()
-        plane_send(idh_out, idh_in, idh_ss, idh_rs, 0, n_z, 6, 2)
+        for region, by in ((7, 4 * cc - 2), (5, -1), (6, 1)):
+            for m in range(plane - 1, -1, -1):
+                device = beside(m, by)
+                pltpu.make_async_remote_copy(
+                    src_ref=idh_out.at[region, device[0] // n_z * n_gy + device[1], pl.ds(6, 2)],
+                    dst_ref=idh_in.at[region, me, pl.ds(6, 2)],
+                    send_sem=idh_ss.at[1],
+                    recv_sem=idh_rs.at[1],
+                    device_id=device,
+                    device_id_type=MESH,
+                ).start()
+        plane_send(idh_out, idh_in, idh_ss.at[0], idh_rs.at[0], 0, 5, 6, 2)
 
     def pick_for_flows():
-        idh_whole.wait_recv()
-        for r in range(n_z):
-            hot = picked(idh_in[:, r]).reshape(plane * 8, 128).astype(BF16)
-            pick_u[r, :, 0:128] = hot
-            pick_u[r, :, 128:256] = hot
+        for whole in idh_whole:
+            whole.wait_recv()
+        for k, (_, _, region, first, step) in enumerate(RELAYS):
+            tiles = idh_in[region]
+            if step == 2:
+                tiles = tiles.reshape(plane // 2, 2, 8, 128)[:, first]
+            keep_pick(pick_u, k, picked(tiles))
 
     def pick_for_bins():
         pick_ht[...] = flat(hot_h).T.astype(BF16)
 
     def pick_for_columns():
-        for g in range(3):
-            plane_whole(idw_out, idw_in, idw_ss, idw_rs.at[g], *GROUPS[g], 6, 2).wait_recv()
-        hot_c = picked(idw_in[...].reshape(plane * n_z, 8, 128))
-        pick_ct[...] = flat(hot_c).T.astype(BF16)
+        for g, (first, tiles) in enumerate(GROUPS):
+            plane_whole(idw_out, idw_in, idw_ss, idw_rs.at[g], first, tiles, 6, 2).wait_recv()
+            held = idw_in[pl.ds(first, tiles)].reshape(tiles * plane, 8, 128)
+            hot_c = picked(held).reshape(tiles * plane * 8, 128)
+            pick_ct[:, columns_of(g)] = hot_c.T.astype(BF16)
 
     def squares():
         tail = flat(w_in[0])
         tail = jnp.where(lax.broadcasted_iota(jnp.int32, tail.shape, 0) % 8 < 6, 0.0, tail)
-        solid_at[2] = collect(pick_ct, tail * tail, False)[96:128]
+        solid_at[2] = collect(pick_ct[...], tail * tail, False)[96:128]
 
     def fluid_first(t):
-        rows = weights[t].receive()
-        table = collect(pick_ct, rows, t > 0)
+        table = weights[t].collected(pick_ct, t > 0)
         if t == 0:
             solid_at[1] = table[96:128]
         parts = [table[a * 32 : a * 32 + 32] for a in range(3)]
@@ -582,19 +641,23 @@
         steps[f"stream{t}"] = lambda t=t: fluid_last(t)
         steps[f"grain{t}"] = lambda t=t: grain(t)
         for name, one in (("w", weights[t]), ("u", flows[t])):
-            ids = send_ids if name == "w" and t == 0 else lambda g: None
-            steps[f"own_{name}{t}"] = lambda one=one, ids=ids: (one.send(0), ids(0))
-            steps[f"on_{name}{t}"] = lambda one=one: one.forward()
-            steps[f"near_{name}{t}"] = lambda one=one, ids=ids: (one.near_parts(), ids(1))
-            steps[f"far_{name}{t}"] = lambda one=one, ids=ids: (one.far_parts(), ids(2))
+            first = name == "w" and t == 0
+            steps[f"own_{name}{t}"] = lambda one=one, first=first: (
+                one.send(0), send_ids(0) if first else None
+            )
+            steps[f"relay_{name}{t}"] = lambda one=one, first=first: (
+                one.relay(), (send_ids_far(), send_ids(1)) if first else None
+            )
 
     pl.semaphore_wait(barrier, len(greeted))
     assert sorted(ORDER) == sorted(steps)
     for name in ORDER:
         steps[name]()
 
-    idh_whole.wait_send()
-    plane_whole(idw_out, idw_in, idw_ss, idw_rs.at[0], 0, n_z, 6, 2).wait_send()
+    for whole in idh_whole:
+        whole.wait_send()
+    for n, (first, tiles) in enumerate([(0, 5), (5, 3)]):
+        plane_whole(idw_out, idw_in, idw_ss.at[n], idw_rs.at[n], first, tiles, 6, 2).wait_send()
     for t in range(SUBSTEPS):
         weights[t].finish()
         flows[t].finish()
@@ -620,26 +683,26 @@
             scratch_shapes=[
                 pltpu.VMEM((608, 128), F32),
                 pltpu.VMEM((608, 128), F32),
-                pltpu.VMEM((8, plane * 8, 256), BF16),
-                pltpu.VMEM((8, plane * 8, 256), BF16),
+                pltpu.VMEM((9, plane * 8, 256), BF16),
+                pltpu.VMEM((9, plane * 8, 256), BF16),
                 pltpu.VMEM((128, plane * 64), BF16),
                 pltpu.VMEM((128, plane * 64), BF16),
             ]
-            + [pltpu.VMEM((plane, 8, 8, 128), F32)] * 4
+            + [pltpu.VMEM((n, plane, 8, 128), F32) for n in (8, 8, 9, 8)]
             + [
-                pltpu.VMEM((SUBSTEPS, 8, 96, 128), F32),
-                pltpu.VMEM((SUBSTEPS, 8, 136, 128), F32),
+                pltpu.VMEM((SUBSTEPS, 5, 96, 128), F32),
+                pltpu.VMEM((SUBSTEPS, 5, 136, 128), F32),
             ]
-            + [pltpu.VMEM((SUBSTEPS, plane, 8, 8, 128), F32)] * 4
+            + [pltpu.VMEM((SUBSTEPS, n, plane, 8, 128), F32) for n in (9, 8, 9, 8)]
             + [
                 pltpu.VMEM((SUBSTEPS, 17, 8, 128), F32),
                 pltpu.VMEM((SUBSTEPS, 25, 8, 128), F32),
-                dma,
-                dma,
-                dma,
+                dma((2,)),
+                dma((2,)),
+                dma((2,)),
                 dma((3,)),
             ]
-            + [dma((SUBSTEPS,)), dma((SUBSTEPS, 9)), dma((SUBSTEPS,)), dma((SUBSTEPS, 3))] * 2
+            + [dma((SUBSTEPS,)), dma((SUBSTEPS, 5)), dma((SUBSTEPS, 2)), dma((SUBSTEPS, 3))] * 2
             + [dma((SUBSTEPS,)), dma((SUBSTEPS,))],
             compiler_params=pltpu.CompilerParams(
                 collective_id=0, has_side_effects=True, vmem_limit_bytes=48 << 20

time: 86.3 us -> 84 us (0.973)
  Pallas kernels: 79.3 us -> 77.1 us
    pallas_call x1, Pallas kernels: 79.3 us -> 77.1 us  [body(): pl.pallas_call(lambda *refs: kernel(n_gx, n_gy, *refs), out_shape=(jax.Sh...]
where the time goes in v4:
time: 84 us; the launch traced here: 83.7 us
  Pallas kernels  77.1 us (92%)
  local copies, waits for them, and re-layouts  5.9 us (7%)
    pallas_call x1, Pallas kernels, body(): pl.pallas_call(lambda *refs: kernel(n_gx, n_gy, *refs), out_shape=(jax.Sh...  77.1 us
    unnamed x14, local copies, waits for them, and re-layouts  5.9 us

profile of v4, /device:TPU:1, one launch (start us, length us, event | category | flops | bytes accessed | tf_op | source)
XLA Modules:
  0.0 83.7 jit_solution(12274705996297039664)
XLA Ops:
  0.6 0.0 copy-start
  0.6 1.0 %copy-done = f32[19,4,8,128]{3,2,1,0:T(8,128)S(1)} copy-done((f32[19,4,8,128]{3,2,1,0:T(8,128)S(1)}, f32[19,4,8,128]{3,2,1,0:T(8,128)}, u32[]{:S(2)}) %copy-start) | copy-done | bytes 311320
  1.6 0.0 copy-start.1
  1.6 0.8 copy-done.1
  2.4 0.0 copy-start.2
  2.4 0.7 copy-done.2
  3.1 0.0 copy-start.3
  3.1 0.7 copy-done.3
  3.8 0.0 copy-start.4
  3.8 0.7 copy-done.4
  4.6 0.0 copy-start.5
  4.6 0.7 copy-done.5
  5.2 77.1 %bed.1 = (f32[19,4,8,128]{3,2,1,0:T(8,128)S(1)}, f32[3,32,128]{2,1,0:T(8,128)S(1)}) custom-call(f32[19,4,8,128]{3,2,1,0:T(8,128)S(1)} %copy-done, f32[3,32,128]{2,1,0:T(8,128)S(1)} %copy-done.1, f32[32,128]{1,0:T(8,128)S(1)} %copy-done.2, s32[32,128]{1,0:T(8,128)S(1)} %copy-done.3, s32[32,32]{1,0:T(8,128)S(1)} %copy-done.4, s32[32]{0:T(128)S(1)} %copy-done.5), custom_call_target="tpu_custom_call" | custom-call | tf_op jit(solution)/shard_map/bed/pallas_call | solution.py:675
  82.3 0.7 copy.10
  83.0 0.6 copy.11
Async XLA Ops:
  0.6 1.0 %copy-start = (f32[19,4,8,128]{3,2,1,0:T(8,128)S(1)}, f32[19,4,8,128]{3,2,1,0:T(8,128)}, u32[]{:S(2)}) copy-start(f32[19,4,8,128]{3,2,1,0:T(8,128)} %refs_0_.1) | copy-start | bytes 933892
  1.6 0.8 copy-start.1
  2.4 0.7 copy-start.2
  3.1 0.7 copy-start.3
  3.8 0.7 copy-start.4
  4.6 0.7 copy-start.5

commit v5 on v4

--- a/solution.py
+++ b/solution.py
@@ -35,8 +35,8 @@
 ]
 
 ORDER = [
-    "start_w0", "own_w0", "relay_w0", "start_u0", "pick_u", "start_w1", "own_u0",
-    "relay_u0", "own_w1", "pick_h", "relay_w1", "pick_c", "collide0", "grain0",
+    "start_w0", "start_u0", "own_w0", "relay_w0", "start_w1", "pick_u", "own_u0",
+    "relay_u0", "own_w1", "pick_h", "pick_c", "relay_w1", "collide0", "grain0",
     "own_w2", "stream0", "own_u1", "squares", "relay_w2", "collide1", "relay_u1",
     "stream1", "own_u2", "collide2", "grain1", "own_w3", "relay_u2", "stream2",
     "relay_w3", "own_u3", "relay_u3", "collide3", "grain2", "grain3", "stream3",

time: 84 us -> 81.2 us (0.967)
  Pallas kernels: 77.1 us -> 74.3 us
    pallas_call x1, Pallas kernels: 77.1 us -> 74.3 us  [body(): pl.pallas_call(lambda *refs: kernel(n_gx, n_gy, *refs), out_shape=(jax.Sh...]
where the time goes in v5:
time: 81.2 us; the launch traced here: 80.9 us
  Pallas kernels  74.3 us (92%)
  local copies, waits for them, and re-layouts  5.9 us (7%)
    pallas_call x1, Pallas kernels, body(): pl.pallas_call(lambda *refs: kernel(n_gx, n_gy, *refs), out_shape=(jax.Sh...  74.3 us
    unnamed x14, local copies, waits for them, and re-layouts  5.9 us

profile of v5, /device:TPU:1, one launch (start us, length us, event | category | flops | bytes accessed | tf_op | source)
XLA Modules:
  0.0 80.9 jit_solution(8872933161979105743)
XLA Ops:
  0.6 0.0 copy-start
  0.6 1.0 %copy-done = f32[19,4,8,128]{3,2,1,0:T(8,128)S(1)} copy-done((f32[19,4,8,128]{3,2,1,0:T(8,128)S(1)}, f32[19,4,8,128]{3,2,1,0:T(8,128)}, u32[]{:S(2)}) %copy-start) | copy-done | bytes 311320
  1.6 0.0 copy-start.1
  1.6 0.8 copy-done.1
  2.4 0.0 copy-start.2
  2.4 0.7 copy-done.2
  3.1 0.0 copy-start.3
  3.1 0.7 copy-done.3
  3.8 0.0 copy-start.4
  3.8 0.7 copy-done.4
  4.6 0.0 copy-start.5
  4.6 0.7 copy-done.5
  5.2 74.3 %bed.1 = (f32[19,4,8,128]{3,2,1,0:T(8,128)S(1)}, f32[3,32,128]{2,1,0:T(8,128)S(1)}) custom-call(f32[19,4,8,128]{3,2,1,0:T(8,128)S(1)} %copy-done, f32[3,32,128]{2,1,0:T(8,128)S(1)} %copy-done.1, f32[32,128]{1,0:T(8,128)S(1)} %copy-done.2, s32[32,128]{1,0:T(8,128)S(1)} %copy-done.3, s32[32,32]{1,0:T(8,128)S(1)} %copy-done.4, s32[32]{0:T(128)S(1)} %copy-done.5), custom_call_target="tpu_custom_call" | custom-call | tf_op jit(solution)/shard_map/bed/pallas_call | solution.py:675
  79.5 0.7 copy.10
  80.2 0.6 copy.11
Async XLA Ops:
  0.6 1.0 %copy-start = (f32[19,4,8,128]{3,2,1,0:T(8,128)S(1)}, f32[19,4,8,128]{3,2,1,0:T(8,128)}, u32[]{:S(2)}) copy-start(f32[19,4,8,128]{3,2,1,0:T(8,128)} %refs_0_.1) | copy-start | bytes 933892
  1.6 0.8 copy-start.1
  2.4 0.7 copy-start.2
  3.1 0.7 copy-start.3
  3.8 0.7 copy-start.4
  4.6 0.7 copy-start.5
